TPU v7x, 32 devices: a whole 2x2x4 slice. The times are simulated.
32 devices in a mesh: dp: 4 (over y, x), ctx: 8 (over z, core).
Axes of the slice: x: 2, y: 2, z: 4, core: 2. Of those that a mesh axis runs over, the one named last changes fastest.
Arguments:
- q_proj: bfloat16 [4, 1024, 2048], P('dp', 'ctx'), may hold values from -80 to 80
- k_proj: bfloat16 [4, 1024, 1024], P('dp', 'ctx'), may hold values from -80 to 80
- v_proj: bfloat16 [4, 1024, 1024], P('dp', 'ctx'), may hold values from -6 to 6
- d_out: bfloat16 [4, 1024, 2048], P('dp', 'ctx'), may hold values from -7 to 7
- q_gain: float32 [128], replicated, may hold values from 0.5 to 9
- k_gain: float32 [128], replicated, may hold values from 0.5 to 9
Outputs:
- attn_out: bfloat16 [4, 1024, 2048], P('dp', 'ctx')
- d_q_proj: bfloat16 [4, 1024, 2048], P('dp', 'ctx')
- d_k_proj: bfloat16 [4, 1024, 1024], P('dp', 'ctx')
- d_v_proj: bfloat16 [4, 1024, 1024], P('dp', 'ctx')
- gain_grads: float32 [256], P('dp')
All inputs are finite; a program needn't handle non-finite values.
Results may differ from a plain program's by a relative error of at most 0.017.
The roundings to bfloat16 on the way count: a program that leaves them out, or rounds other values in their place, can miss the bound.
Values may be sent and summed in bfloat16 or wider, within the bound.
No kernel may reach another device: no remote copies, remote signals or barrier semaphores. Data moves between devices by JAX's collectives and lax.ppermute only.
A program may use at most 64 MiB of HBM per device.

v0:
```python
import jax
import jax.numpy as jnp
from jax import lax
from jax.sharding import PartitionSpec as P

WINDOW = 256


EPSILON = 1e-06
ROPE_BASE = 10000.0
SCORE_SCALE = 168.0 ** (-0.5)


def shifted(value, axis, steps):
    count = lax.axis_size(axis)
    initial, last = (max(0, -steps), min(count, count - steps))
    return lax.ppermute(value, axis, [(source, source + steps) for source in range(initial, last)])


def norm_rope(values, gain, positions):
    mean_sq = jnp.mean(values * values, axis=-1, keepdims=True)
    normed = values * lax.rsqrt(mean_sq + EPSILON) * gain
    half_size = values.shape[-1] // 2
    freqs = jnp.power(ROPE_BASE, -2.0 * jnp.arange(half_size, dtype=jnp.float32) / values.shape[-1])
    angles = positions.astype(jnp.float32)[:, None, None] * freqs
    cosine = jnp.cos(angles)
    sine = jnp.sin(angles)
    first = normed[..., :half_size]
    second = normed[..., half_size:]
    return jnp.concatenate(
        [first * cosine - second * sine, second * cosine + first * sine], axis=-1
    )


def attend(queries, keys, values, grad_out, visible):
    scores = (
        jnp.einsum("kqd,ked->kqe", queries, keys, preferred_element_type=jnp.float32) * SCORE_SCALE
    )
    masked = jnp.where(visible[None], scores, -1e30)
    highest = jnp.max(masked, axis=-1, keepdims=True)
    exponent = jnp.exp(masked - highest)
    probabilities = exponent / jnp.sum(exponent, axis=-1, keepdims=True)
    probs_b = probabilities.astype(jnp.bfloat16)
    result = jnp.einsum("kqe,ked->kqd", probs_b, values, preferred_element_type=jnp.float32)
    d_prob = jnp.einsum("kqd,ked->kqe", grad_out, values, preferred_element_type=jnp.float32)
    delta = jnp.sum(probabilities * d_prob, axis=-1, keepdims=True)
    d_score = (probabilities * (d_prob - delta) * SCORE_SCALE).astype(jnp.bfloat16)
    d_query = jnp.einsum("kqe,ked->kqd", d_score, keys, preferred_element_type=jnp.float32)
    d_key = jnp.einsum("kqe,kqd->ked", d_score, queries, preferred_element_type=jnp.float32)
    d_value = jnp.einsum("kqe,kqd->ked", probs_b, grad_out, preferred_element_type=jnp.float32)
    return (result, d_query, d_key, d_value)


def head_major(rows, tok_rows, heads, group_size, head_size):
    return (
        rows.reshape(tok_rows, heads, group_size, head_size)
        .transpose(1, 2, 0, 3)
        .reshape(heads, group_size * tok_rows, head_size)
    )


def token_major(blocks_in, tok_rows, heads, group_size, head_size):
    return (
        blocks_in.reshape(heads, group_size, tok_rows, head_size)
        .transpose(2, 0, 1, 3)
        .reshape(tok_rows, heads * group_size * head_size)
    )


def on_device(q_proj, k_proj, v_proj, d_out, q_gain, k_gain):
    tok_rows = q_proj.shape[1]
    head_size = q_gain.shape[0]
    q_heads = q_proj.shape[2] // head_size
    kv_heads = k_proj.shape[2] // head_size
    group_size = q_heads // kv_heads
    width = kv_heads * head_size
    first_row = lax.axis_index("ctx") * tok_rows
    positions = first_row + jnp.arange(tok_rows, dtype=jnp.int32)
    q_float = q_proj[0].astype(jnp.float32).reshape(tok_rows, q_heads, head_size)
    k_float = k_proj[0].astype(jnp.float32).reshape(tok_rows, kv_heads, head_size)
    q_rot = (
        norm_rope(q_float, q_gain, positions)
        .astype(jnp.bfloat16)
        .reshape(tok_rows, q_heads * head_size)
    )
    k_rot = norm_rope(k_float, k_gain, positions).astype(jnp.bfloat16).reshape(tok_rows, width)
    own_rows = jnp.concatenate([k_rot, v_proj[0]], axis=1)
    blocks = WINDOW // tok_rows
    pieces = []
    for hop_count in range(1, blocks + 1):
        outgoing = own_rows if hop_count < blocks else own_rows[1:]
        pieces.append(shifted(outgoing, "ctx", hop_count))
    farthest = jnp.concatenate([jnp.zeros((1, 2 * width), jnp.bfloat16), pieces[-1]], axis=0)
    extended = jnp.concatenate([farthest] + pieces[-2::-1] + [own_rows], axis=0)
    key_span = extended.shape[0]
    row_ids = jnp.arange(tok_rows, dtype=jnp.int32)[:, None]
    key_ids = jnp.arange(key_span, dtype=jnp.int32)[None, :]
    visible = (
        (key_ids > row_ids) & (key_ids <= row_ids + WINDOW) & (key_ids + first_row - WINDOW >= 0)
    )
    visible_rows = jnp.tile(visible, (group_size, 1))
    pair_heads = 2
    pair_width = pair_heads * head_size
    results = []
    query_grads = []
    key_grads = []
    value_grads = []
    for pair_index in range(kv_heads // pair_heads):
        low = pair_index * pair_width
        queries = head_major(
            q_rot[:, low * group_size : (low + pair_width) * group_size],
            tok_rows,
            pair_heads,
            group_size,
            head_size,
        )
        grad_out = head_major(
            d_out[0][:, low * group_size : (low + pair_width) * group_size],
            tok_rows,
            pair_heads,
            group_size,
            head_size,
        )
        keys = (
            extended[:, low : low + pair_width]
            .reshape(key_span, pair_heads, head_size)
            .transpose(1, 0, 2)
        )
        values = (
            extended[:, width + low : width + low + pair_width]
            .reshape(key_span, pair_heads, head_size)
            .transpose(1, 0, 2)
        )
        result, d_query, d_key, d_value = attend(queries, keys, values, grad_out, visible_rows)
        results.append(token_major(result, tok_rows, pair_heads, group_size, head_size))
        query_grads.append(token_major(d_query, tok_rows, pair_heads, group_size, head_size))
        key_grads.append(d_key.transpose(1, 0, 2).reshape(key_span, pair_width))
        value_grads.append(d_value.transpose(1, 0, 2).reshape(key_span, pair_width))
    attn_rows = jnp.concatenate(results, axis=1).astype(jnp.bfloat16)
    d_q_rot = jnp.concatenate(query_grads, axis=1).reshape(tok_rows, q_heads, head_size)
    grads_ext = jnp.concatenate(key_grads + value_grads, axis=1)
    summed = grads_ext[WINDOW:]
    for hop_count in range(1, blocks + 1):
        grad_block = grads_ext[
            WINDOW - hop_count * tok_rows : WINDOW - (hop_count - 1) * tok_rows
        ].astype(jnp.bfloat16)
        if hop_count == blocks:
            grad_block = grad_block[1:]
        arrived = shifted(grad_block, "ctx", -hop_count).astype(jnp.float32)
        if hop_count == blocks:
            arrived = jnp.concatenate([jnp.zeros((1, 2 * width), jnp.float32), arrived], axis=0)
        summed = summed + arrived
    d_k_rot = summed[:, :width].reshape(tok_rows, kv_heads, head_size)
    d_value_rows = summed[:, width:].astype(jnp.bfloat16)

    def rotate_side(values, gain):
        return norm_rope(values, gain, positions)

    _, q_back = jax.vjp(rotate_side, q_float, q_gain)
    d_q_in, d_q_gain = q_back(d_q_rot)
    _, k_back = jax.vjp(rotate_side, k_float, k_gain)
    d_k_in, d_k_gain = k_back(d_k_rot)
    gain_terms = jnp.concatenate([d_q_gain, d_k_gain])
    gathered_terms = lax.psum(gain_terms, "ctx")
    gain_share = lax.psum_scatter(gathered_terms, "dp", scatter_dimension=0, tiled=True)
    return (
        attn_rows[None],
        d_q_in.astype(jnp.bfloat16).reshape(1, tok_rows, q_heads * head_size),
        d_k_in.astype(jnp.bfloat16).reshape(1, tok_rows, width),
        d_value_rows[None],
        gain_share,
    )


def solution(mesh):
    return jax.shard_map(
        on_device,
        mesh=mesh,
        in_specs=(
            P("dp", "ctx", None),
            P("dp", "ctx", None),
            P("dp", "ctx", None),
            P("dp", "ctx", None),
            P(),
            P(),
        ),
        out_specs=(
            P("dp", "ctx", None),
            P("dp", "ctx", None),
            P("dp", "ctx", None),
            P("dp", "ctx", None),
            P("dp"),
        ),
        check_vma=False,
    )
```

profile of v0, /device:TPU:0, one launch (start us, length us, event | category | flops | bytes accessed | tf_op | source)
XLA Modules:
  0.0 182.8 jit_solution(1735053363875596797)
XLA Ops:
  5.4 3.2 %collective-permute-start.1 = (bf16[128,2048]{0,1:T(8,128)(2,1)}, bf16[128,2048]{0,1:T(8,128)(2,1)}, u32[]{:S(2)}, u32[]{:S(2)}) collective-permute-start(bf16[128,2048]{0,1:T(8,128)(2,1)} %pad_maximum_fusion.1), channel_id=1, source_target_pairs={{0,1},{1,2},{2,3},{3,4},{4,5},{5,6},{6,7},{8,9},{9,10},{10,11},{11... | collective-permute-start | bytes 1572872 | tf_op jit(solution)/shard_map/ppermute | solution.py:17
  9.5 4.6 %collective-permute-start = (bf16[127,2048]{0,1:T(8,128)(2,1)}, bf16[127,2048]{0,1:T(8,128)(2,1)}, u32[]{:S(2)}, u32[]{:S(2)}) collective-permute-start(bf16[127,2048]{0,1:T(8,128)(2,1)} %fusion.62), channel_id=1, source_target_pairs={{0,2},{1,3},{2,4},{3,5},{4,6},{5,7},{8,10},{9,11},{10,12},{11,13},... | collective-permute-start | bytes 1560584 | tf_op jit(solution)/shard_map/ppermute | solution.py:17
  33.9 2.3 %fusion.190 = (f32[2,256]{1,0:T(2,128)S(1)}, f32[2,256,384]{2,1,0:T(8,128)}) fusion(bf16[2,256,128]{2,1,0:T(8,128)(2,1)} %bitcast.307, pred[256,384]{1,0:T(8,128)(4,1)S(1)} %bitcast.311, bf16[384,2,128]{2,0,1:T(8,128)(2,1)} %copy.210), kind=kOutput, calls=%fused_computation.204 | convolution fusion | flops 51118464 | bytes 1214464 | tf_op jit(solution)/shard_map/sub | solution.py:41
  36.2 2.6 %convolution_convert_fusion.2 = bf16[2,256,128]{2,1,0:T(8,128)(2,1)} fusion(bf16[384,2,128]{2,0,1:T(8,128)(2,1)S(1)} %copy.211, f32[2,256]{1,0:T(2,128)S(1)} %get-tuple-element.39, bf16[2,256,128]{2,1,0:T(8,128)(2,1)} %bitcast.308, pred[256,384]{1,0:T(8,128)(4,1)S(1)} %bitcast.312, bf16[384,2,128]{2,0,1:T(8,128)(2,1)} %copy.210), kind=kOutput, calls=%fused_computation.48 | convolution fusion | flops 101712768 | bytes 755712 | tf_op jit(solution)/shard_map/kqe,ked->kqd/dot_general | solution.py:44
  38.9 5.2 %fusion.49 = f32[2,256,128]{2,1,0:T(8,128)} fusion(f32[2,256,384]{2,1,0:T(8,128)} %convolution_bitcast_fusion.2, bf16[384,2,128]{2,0,1:T(8,128)(2,1)} %copy.210, f32[2,256,384]{2,1,0:T(8,128)} %get-tuple-element.40, f32[2,256]{1,0:T(2,128)} %copy-done.25), kind=kOutput, calls=%fused_computation.61 | convolution fusion | flops 51708800 | bytes 2033664 | tf_op jit(solution)/shard_map/kqe,ked->kqd/dot_general | solution.py:48
  44.1 5.4 %fusion.48 = f32[2,384,128]{1,2,0:T(8,128)} fusion(bf16[2,256,128]{2,1,0:T(8,128)(2,1)} %bitcast.309, f32[2,256,384]{2,1,0:T(8,128)} %convolution_bitcast_fusion.2, f32[2,256,384]{2,1,0:T(8,128)} %get-tuple-element.40, f32[2,256]{1,0:T(2,128)S(1)} %copy-done.26), kind=kOutput, calls=%fused_computation.60 | convolution fusion | flops 51708800 | bytes 2099200 | tf_op jit(solution)/shard_map/kqe,kqd->ked/dot_general | solution.py:49
  49.5 2.8 %fusion.95 = f32[2,384,128]{1,2,0:T(8,128)} fusion(bf16[2,256,128]{2,1,0:T(8,128)(2,1)S(1)} %bitcast.273, f32[2,256]{1,0:T(2,128)S(1)} %copy-done.26, bf16[2,256,128]{2,1,0:T(8,128)(2,1)} %bitcast.310, pred[256,384]{1,0:T(8,128)(4,1)} %bitcast.313, bf16[384,2,128]{2,0,1:T(8,128)(2,1)S(1)} %copy-done.13), kind=kOutput, calls=%fused_computation.140 | convolution fusion | flops 101647232 | bytes 952320 | tf_op jit(solution)/shard_map/kqe,kqd->ked/dot_general | solution.py:50
  55.2 2.9 %fusion.187 = (f32[2,256]{1,0:T(2,128)}, f32[2,256,384]{2,1,0:T(8,128)}) fusion(bf16[2,256,128]{2,1,0:T(8,128)(2,1)} %bitcast.303, pred[256,384]{1,0:T(8,128)(4,1)} %bitcast.314, bf16[384,2,128]{2,0,1:T(8,128)(2,1)} %copy.214), kind=kOutput, calls=%fused_computation.203 | convolution fusion | flops 51118464 | bytes 1214464 | tf_op jit(solution)/shard_map/sub | solution.py:41
  58.2 2.8 %convolution_convert_fusion.1 = bf16[2,256,128]{2,1,0:T(8,128)(2,1)} fusion(bf16[384,2,128]{2,0,1:T(8,128)(2,1)} %copy.215, f32[2,256]{1,0:T(2,128)} %get-tuple-element.37, bf16[2,256,128]{2,1,0:T(8,128)(2,1)} %bitcast.304, pred[256,384]{1,0:T(8,128)(4,1)} %bitcast.315, bf16[384,2,128]{2,0,1:T(8,128)(2,1)} %copy.214), kind=kOutput, calls=%fused_computation.47 | convolution fusion | flops 101712768 | bytes 755712 | tf_op jit(solution)/shard_map/kqe,ked->kqd/dot_general | solution.py:44
  61.0 4.6 %fusion.43 = f32[2,256,128]{2,1,0:T(8,128)} fusion(f32[2,256,384]{2,1,0:T(8,128)S(1)} %convolution_bitcast_fusion.1, bf16[384,2,128]{2,0,1:T(8,128)(2,1)} %copy.214, f32[2,256,384]{2,1,0:T(8,128)} %get-tuple-element.38, f32[2,256]{1,0:T(2,128)} %get-tuple-element.37), kind=kOutput, calls=%fused_computation.56 | convolution fusion | flops 51708800 | bytes 2033664 | tf_op jit(solution)/shard_map/kqe,ked->kqd/dot_general | solution.py:48
  65.6 4.9 %fusion.42 = f32[2,384,128]{1,2,0:T(8,128)} fusion(bf16[2,256,128]{2,1,0:T(8,128)(2,1)} %bitcast.305, f32[2,256,384]{2,1,0:T(8,128)S(1)} %convolution_bitcast_fusion.1, f32[2,256,384]{2,1,0:T(8,128)} %get-tuple-element.38, f32[2,256]{1,0:T(2,128)} %get-tuple-element.37), kind=kOutput, calls=%fused_computation.55 | convolution fusion | flops 51708800 | bytes 2099200 | tf_op jit(solution)/shard_map/kqe,kqd->ked/dot_general | solution.py:49
  70.5 3.0 %fusion.92 = f32[2,384,128]{1,2,0:T(8,128)} fusion(bf16[2,256,128]{2,1,0:T(8,128)(2,1)} %bitcast.271, f32[2,256]{1,0:T(2,128)} %get-tuple-element.37, bf16[2,256,128]{2,1,0:T(8,128)(2,1)} %bitcast.306, pred[256,384]{1,0:T(8,128)(4,1)} %bitcast.316, bf16[384,2,128]{2,0,1:T(8,128)(2,1)} %copy.214), kind=kOutput, calls=%fused_computation.137 | convolution fusion | flops 101647232 | bytes 952320 | tf_op jit(solution)/shard_map/kqe,kqd->ked/dot_general | solution.py:50
  74.8 2.3 %fusion.184 = (f32[2,256]{1,0:T(2,128)S(1)}, f32[2,256,384]{2,1,0:T(8,128)}) fusion(bf16[2,256,128]{2,1,0:T(8,128)(2,1)} %bitcast.298, pred[256,384]{1,0:T(8,128)(4,1)} %bitcast.317, bf16[384,2,128]{2,0,1:T(8,128)(2,1)} %copy.218), kind=kOutput, calls=%fused_computation.202 | convolution fusion | flops 51118464 | bytes 1214464 | tf_op jit(solution)/shard_map/sub | solution.py:41
  77.1 2.9 %convolution_convert_fusion = bf16[2,256,128]{2,1,0:T(8,128)(2,1)} fusion(bf16[384,2,128]{2,0,1:T(8,128)(2,1)S(1)} %copy.219, f32[2,256]{1,0:T(2,128)S(1)} %get-tuple-element.35, bf16[2,256,128]{2,1,0:T(8,128)(2,1)} %bitcast.299, pred[256,384]{1,0:T(8,128)(4,1)} %bitcast.318, bf16[384,2,128]{2,0,1:T(8,128)(2,1)} %copy.218), kind=kOutput, calls=%fused_computation.46 | convolution fusion | flops 101712768 | bytes 755712 | tf_op jit(solution)/shard_map/kqe,ked->kqd/dot_general | solution.py:44
  80.0 4.7 %fusion.37 = f32[2,256,128]{2,1,0:T(8,128)} fusion(f32[2,256,384]{2,1,0:T(8,128)S(1)} %convolution_bitcast_fusion, bf16[384,2,128]{2,0,1:T(8,128)(2,1)} %copy.218, f32[2,256,384]{2,1,0:T(8,128)} %get-tuple-element.36, f32[2,256]{1,0:T(2,128)S(1)} %get-tuple-element.35), kind=kOutput, calls=%fused_computation.51 | convolution fusion | flops 51708800 | bytes 2033664 | tf_op jit(solution)/shard_map/kqe,ked->kqd/dot_general | solution.py:48
  84.6 4.9 %fusion.36 = f32[2,384,128]{1,2,0:T(8,128)} fusion(bf16[2,256,128]{2,1,0:T(8,128)(2,1)} %bitcast.300, f32[2,256,384]{2,1,0:T(8,128)S(1)} %convolution_bitcast_fusion, f32[2,256,384]{2,1,0:T(8,128)} %get-tuple-element.36, f32[2,256]{1,0:T(2,128)S(1)} %get-tuple-element.35), kind=kOutput, calls=%fused_computation.50 | convolution fusion | flops 51708800 | bytes 2099200 | tf_op jit(solution)/shard_map/kqe,kqd->ked/dot_general | solution.py:49
  89.5 2.8 %fusion.89 = f32[2,384,128]{1,2,0:T(8,128)} fusion(bf16[2,256,128]{2,1,0:T(8,128)(2,1)S(1)} %bitcast.269, f32[2,256]{1,0:T(2,128)S(1)} %get-tuple-element.35, bf16[2,256,128]{2,1,0:T(8,128)(2,1)} %bitcast.301, pred[256,384]{1,0:T(8,128)(4,1)} %bitcast.319, bf16[384,2,128]{2,0,1:T(8,128)(2,1)S(1)} %copy-done.14), kind=kOutput, calls=%fused_computation.134 | convolution fusion | flops 101647232 | bytes 952320 | tf_op jit(solution)/shard_map/kqe,kqd->ked/dot_general | solution.py:50
  95.2 2.6 %convolution_convert_fusion.3 = bf16[2,256,128]{2,1,0:T(8,128)(2,1)} fusion(bf16[384,2,128]{2,0,1:T(8,128)(2,1)S(1)} %copy.207, f32[2,256]{1,0:T(2,128)S(1)} %get-tuple-element.41, bf16[2,256,128]{2,1,0:T(8,128)(2,1)} %bitcast.294, pred[256,384]{1,0:T(8,128)(4,1)} %bitcast.321, bf16[384,2,128]{2,0,1:T(8,128)(2,1)S(1)} %copy.206), kind=kOutput, calls=%fused_computation.49 | convolution fusion | flops 101712768 | bytes 755712 | tf_op jit(solution)/shard_map/kqe,ked->kqd/dot_general | solution.py:44
  97.8 2.8 %fusion.98 = f32[2,384,128]{1,2,0:T(8,128)} fusion(bf16[2,256,128]{2,1,0:T(8,128)(2,1)S(1)} %bitcast.267, f32[2,256]{1,0:T(2,128)S(1)} %get-tuple-element.41, bf16[2,256,128]{2,1,0:T(8,128)(2,1)} %bitcast.295, pred[256,384]{1,0:T(8,128)(4,1)} %bitcast.322, bf16[384,2,128]{2,0,1:T(8,128)(2,1)S(1)} %copy.206), kind=kOutput, calls=%fused_computation.143 | convolution fusion | flops 101647232 | bytes 952320 | tf_op jit(solution)/shard_map/kqe,kqd->ked/dot_general | solution.py:50
  100.6 4.7 %fusion.55 = f32[2,256,128]{2,1,0:T(8,128)} fusion(f32[2,256,384]{2,1,0:T(8,128)S(1)} %convolution_bitcast_fusion.3, bf16[384,2,128]{2,0,1:T(8,128)(2,1)S(1)} %copy.206, f32[2,256,384]{2,1,0:T(8,128)} %get-tuple-element.42, f32[2,256]{1,0:T(2,128)} %copy-done.24), kind=kOutput, calls=%fused_computation.66 | convolution fusion | flops 51708800 | bytes 2033664 | tf_op jit(solution)/shard_map/kqe,ked->kqd/dot_general | solution.py:48
  105.3 4.9 %fusion.54 = f32[2,384,128]{1,2,0:T(8,128)} fusion(bf16[2,256,128]{2,1,0:T(8,128)(2,1)S(1)} %bitcast.296, f32[2,256,384]{2,1,0:T(8,128)S(1)} %convolution_bitcast_fusion.3, f32[2,256,384]{2,1,0:T(8,128)} %get-tuple-element.42, f32[2,256]{1,0:T(2,128)} %copy-done.24), kind=kOutput, calls=%fused_computation.65 | convolution fusion | flops 51708800 | bytes 2099200 | tf_op jit(solution)/shard_map/kqe,kqd->ked/dot_general | solution.py:49
  143.6 10.1 %collective-permute-done.3 = bf16[127,2048]{1,0:T(8,128)(2,1)} collective-permute-done((bf16[127,2048]{1,0:T(8,128)(2,1)}, bf16[127,2048]{1,0:T(8,128)(2,1)}, u32[]{:S(2)}, u32[]{:S(2)}) %collective-permute-start.3) | collective-permute-done | bytes 520224 | tf_op jit(solution)/shard_map/ppermute | solution.py:17
  157.2 9.9 %all-reduce.5 = f32[256]{0:T(256)S(1)} all-reduce(f32[256]{0:T(256)S(1)} %pad_maximum_fusion.5), channel_id=2, replica_groups=mesh['dp'=4,'ctx'=8] {'dp'}, use_global_device_ids=true, to_apply=%region_19.20.clone | all-reduce | flops 256 | bytes 2048
  167.2 14.1 %psum.8 = f32[64]{0:T(128)} all-reduce(f32[64]{0:T(128)S(1)} %dynamic-slice.1), channel_id=1, replica_groups=mesh['dp'=4,'ctx'=8] {'ctx'}, use_global_device_ids=true, to_apply=%region_18.19 | all-reduce | flops 64 | bytes 512 | tf_op jit(solution)/shard_map/psum | solution.py:164
  (173 shorter events, 69.6 us)
Async XLA Ops:
  0.6 3.0 %copy-start.21 = (f32[128]{0:T(128)S(1)}, f32[128]{0:T(128)}, u32[]{:S(2)}) copy-start(f32[128]{0:T(128)} %param.11) | copy-start | bytes 1540
  3.6 10.5 %copy-start.6 = (bf16[1,128,2048]{2,1,0:T(8,128)(2,1)S(1)}, bf16[1,128,2048]{2,1,0:T(8,128)(2,1)}, u32[]{:S(2)}) copy-start(bf16[1,128,2048]{2,1,0:T(8,128)(2,1)} %param.9) | copy-start | bytes 1572868
  3.8 11.1 %copy-start.3 = (bf16[1,128,2048]{2,1,0:T(8,128)(2,1)S(1)}, bf16[1,128,2048]{2,1,0:T(8,128)(2,1)}, u32[]{:S(2)}) copy-start(bf16[1,128,2048]{2,1,0:T(8,128)(2,1)} %param.6) | copy-start | bytes 1572868
  5.4 22.7 %collective-permute-start.1 = (bf16[128,2048]{0,1:T(8,128)(2,1)}, bf16[128,2048]{0,1:T(8,128)(2,1)}, u32[]{:S(2)}, u32[]{:S(2)}) collective-permute-start(bf16[128,2048]{0,1:T(8,128)(2,1)} %pad_maximum_fusion.1), channel_id=1, source_target_pairs={{0,1},{1,2},{2,3},{3,4},{4,5},{5,6},{6,7},{8,9},{9,10},{10,11},{11... | collective-permute-start | bytes 1572872 | tf_op jit(solution)/shard_map/ppermute | solution.py:17
  9.5 6.2 %copy-start.20 = (f32[128]{0:T(128)S(1)}, f32[128]{0:T(128)}, u32[]{:S(2)}) copy-start(f32[128]{0:T(128)} %param.10) | copy-start | bytes 1540
  9.5 18.5 %collective-permute-start = (bf16[127,2048]{0,1:T(8,128)(2,1)}, bf16[127,2048]{0,1:T(8,128)(2,1)}, u32[]{:S(2)}, u32[]{:S(2)}) collective-permute-start(bf16[127,2048]{0,1:T(8,128)(2,1)} %fusion.62), channel_id=1, source_target_pairs={{0,2},{1,3},{2,4},{3,5},{4,6},{5,7},{8,10},{9,11},{10,12},{11,13},... | collective-permute-start | bytes 1560584 | tf_op jit(solution)/shard_map/ppermute | solution.py:17
  33.9 5.0 %copy-start.19 = (pred[2,128,384]{2,1,0:T(8,128)(4,1)}, pred[2,128,384]{2,1,0:T(8,128)(4,1)S(1)}, u32[]{:S(2)}) copy-start(pred[2,128,384]{2,1,0:T(8,128)(4,1)S(1)} %tile.8) | copy-start | bytes 294916
  36.2 2.7 %copy-start.25 = (f32[2,256]{1,0:T(2,128)}, f32[2,256]{1,0:T(2,128)S(1)}, u32[]{:S(2)}) copy-start(f32[2,256]{1,0:T(2,128)S(1)} %get-tuple-element.39) | copy-start | bytes 6148
  38.9 5.2 %copy-start.26 = (f32[2,256]{1,0:T(2,128)S(1)}, f32[2,256]{1,0:T(2,128)}, u32[]{:S(2)}) copy-start(f32[2,256]{1,0:T(2,128)} %copy-done.25) | copy-start | bytes 6148
  38.9 10.6 %copy-start.5 = (bf16[128,2,2,128]{3,0,2,1:T(8,128)(2,1)S(1)}, bf16[128,2,2,128]{3,0,2,1:T(8,128)(2,1)}, u32[]{:S(2)}) copy-start(bf16[128,2,2,128]{3,0,2,1:T(8,128)(2,1)} %copy.224) | copy-start | bytes 393220
  38.9 10.6 %copy-start.13 = (bf16[384,2,128]{2,0,1:T(8,128)(2,1)S(1)}, bf16[384,2,128]{2,0,1:T(8,128)(2,1)}, u32[]{:S(2)}) copy-start(bf16[384,2,128]{2,0,1:T(8,128)(2,1)} %copy.210) | copy-start | bytes 589828
  70.5 4.0 %copy-start.4 = (bf16[128,2,2,128]{3,0,2,1:T(8,128)(2,1)S(1)}, bf16[128,2,2,128]{3,0,2,1:T(8,128)(2,1)}, u32[]{:S(2)}) copy-start(bf16[128,2,2,128]{3,0,2,1:T(8,128)(2,1)} %copy.230) | copy-start | bytes 393220
  80.0 9.6 %copy-start.14 = (bf16[384,2,128]{2,0,1:T(8,128)(2,1)S(1)}, bf16[384,2,128]{2,0,1:T(8,128)(2,1)}, u32[]{:S(2)}) copy-start(bf16[384,2,128]{2,0,1:T(8,128)(2,1)} %copy.218) | copy-start | bytes 589828
  95.2 5.4 %copy-start.24 = (f32[2,256]{1,0:T(2,128)}, f32[2,256]{1,0:T(2,128)S(1)}, u32[]{:S(2)}) copy-start(f32[2,256]{1,0:T(2,128)S(1)} %get-tuple-element.41) | copy-start | bytes 6148
  100.6 4.7 %copy-start.17 = (bf16[2,2,128,128]{3,2,1,0:T(8,128)(2,1)S(1)}, bf16[2,2,128,128]{3,2,1,0:T(8,128)(2,1)}, u32[]{:S(2)}) copy-start(bf16[2,2,128,128]{3,2,1,0:T(8,128)(2,1)} %copy.201) | copy-start | bytes 393220
  100.6 9.6 %copy-start.8 = (f32[2,384,128]{1,2,0:T(8,128)S(1)}, f32[2,384,128]{1,2,0:T(8,128)}, u32[]{:S(2)}) copy-start(f32[2,384,128]{1,2,0:T(8,128)} %fusion.95) | copy-start | bytes 1179652
  105.3 5.1 %copy-start.7 = (f32[2,384,128]{1,2,0:T(8,128)S(1)}, f32[2,384,128]{1,2,0:T(8,128)}, u32[]{:S(2)}) copy-start(f32[2,384,128]{1,2,0:T(8,128)} %fusion.48) | copy-start | bytes 1179652
  120.5 3.3 %copy-start.2 = (f32[384,256]{1,0:T(8,128)S(1)}, f32[384,256]{1,0:T(8,128)}, u32[]{:S(2)}) copy-start(f32[384,256]{1,0:T(8,128)} %copy.247) | copy-start | bytes 1179652
  124.1 2.7 %copy-start.12 = (f32[2,256,128]{2,1,0:T(8,128)S(1)}, f32[2,256,128]{2,1,0:T(8,128)}, u32[]{:S(2)}) copy-start(f32[2,256,128]{2,1,0:T(8,128)} %fusion.55) | copy-start | bytes 786436
  127.6 5.9 %copy-start.15 = (bf16[2,256,128]{2,1,0:T(8,128)(2,1)S(1)}, bf16[2,256,128]{2,1,0:T(8,128)(2,1)}, u32[]{:S(2)}) copy-start(bf16[2,256,128]{2,1,0:T(8,128)(2,1)} %convolution_convert_fusion.2) | copy-start | bytes 393220
  127.6 6.1 %copy-start.16 = (bf16[2,256,128]{2,1,0:T(8,128)(2,1)S(1)}, bf16[2,256,128]{2,1,0:T(8,128)(2,1)}, u32[]{:S(2)}) copy-start(bf16[2,256,128]{2,1,0:T(8,128)(2,1)} %convolution_convert_fusion.1) | copy-start | bytes 393220
  127.7 7.0 %copy-start.18 = (bf16[2,256,128]{2,1,0:T(8,128)(2,1)S(1)}, bf16[2,256,128]{2,1,0:T(8,128)(2,1)}, u32[]{:S(2)}) copy-start(bf16[2,256,128]{2,1,0:T(8,128)(2,1)} %convolution_convert_fusion) | copy-start | bytes 393220
  130.1 23.6 %collective-permute-start.2 = (bf16[128,2048]{1,0:T(8,128)(2,1)}, bf16[128,2048]{1,0:T(8,128)(2,1)}, u32[]{:S(2)}, u32[]{:S(2)}) collective-permute-start(bf16[128,2048]{1,0:T(8,128)(2,1)} %slice.132), channel_id=1, source_target_pairs={{1,0},{2,1},{3,2},{4,3},{5,4},{6,5},{7,6},{9,8},{10,9},{11,10},{12... | collective-permute-start | bytes 1572872 | tf_op jit(solution)/shard_map/ppermute | solution.py:17
  131.4 22.3 %collective-permute-start.3 = (bf16[127,2048]{1,0:T(8,128)(2,1)}, bf16[127,2048]{1,0:T(8,128)(2,1)}, u32[]{:S(2)}, u32[]{:S(2)}) collective-permute-start(bf16[127,2048]{1,0:T(8,128)(2,1)} %slice.133), channel_id=1, source_target_pairs={{2,0},{3,1},{4,2},{5,3},{6,4},{7,5},{10,8},{11,9},{12,10},{13,11},... | collective-permute-start | bytes 1560584 | tf_op jit(solution)/shard_map/ppermute | solution.py:17
  (7 other events, 12.0 us)
where the time goes:
time: 184 us; the launch traced here: 183 us
  matrix products  75.3 us (41%)
  local copies, waits for them, and re-layouts  42.7 us (23%)
  blocking collectives  24 us (13%)
  other arithmetic  18 us (10%)
  starting transfers between devices  10.6 us (6%)
  waiting for transfers between devices  10.1 us (5%)
  between operations  2.02 us (1%)
    dot_general x4, matrix products, attend(): jnp.einsum('kqe,kqd->ked', d_score, queries, preferred_element_type=jnp.f...  20.1 us
    dot_general x4, matrix products, attend(): jnp.einsum('kqe,ked->kqd', d_score, keys, preferred_element_type=jnp.floa...  19.2 us
    psum x1, blocking collectives, on_device(): gathered_terms = lax.psum(gain_terms, 'ctx')  14.1 us
    dot_general x4, matrix products, attend(): jnp.einsum('kqe,kqd->ked', probs_b, grad_out, preferred_element_type=jnp....  11.4 us
    dot_general x4, matrix products, attend(): jnp.einsum('kqe,ked->kqd', probs_b, values, preferred_element_type=jnp.fl...  10.9 us
    ppermute x4, starting transfers between devices, shifted(): lax.ppermute(value, axis, [(source, source + steps) for source in range(i...  10.6 us
    ppermute x4, waiting for transfers between devices, shifted(): lax.ppermute(value, axis, [(source, source + steps) for source in range(i...  10.1 us
    unnamed x1, blocking collectives  9.92 us
  transfers between devices with their start and end apart: 4, of which 1 were waited for; matrix products, arithmetic and copies ran while one was open for 14% of the time, Pallas kernels for 0%

commit v1 on v0

v1 whole, which is shorter than its diff:
```python
import math

import jax
import jax.numpy as jnp
from jax import lax
from jax.experimental import pallas as pl
from jax.experimental.pallas import tpu as pltpu
from jax.sharding import PartitionSpec as P

WINDOW = 256
EPSILON = 1e-06
ROPE_BASE = 10000.0
SCORE_SCALE = 168.0 ** (-0.5)
LOG2_SCALE = SCORE_SCALE * math.log2(math.e)
HIDDEN = -1e30
GROUP = 2
F32 = jnp.float32
BF16 = jnp.bfloat16


def hop(value, steps):
    count = lax.axis_size("ctx")
    initial, last = (max(0, -steps), min(count, count - steps))
    return lax.ppermute(value, "ctx", [(i, i + steps) for i in range(initial, last)])


def unit(x):
    inverse = lax.rsqrt(jnp.mean(x * x, axis=-1, keepdims=True) + EPSILON)
    return x * inverse, inverse


def rotate(y, cosine, sine):
    return y * cosine + pltpu.roll(y, y.shape[-1] // 2, 1) * sine


def unrotate(d, cosine, sine):
    return d * cosine + pltpu.roll(d * sine, d.shape[-1] // 2, 1)


def unit_back(d_y, normed, inverse, gain):
    d_normed = d_y * gain
    return inverse * (d_normed - normed * jnp.mean(d_normed * normed, axis=-1, keepdims=True))


def fold(x):
    return jnp.sum(x.reshape(-1, 8, x.shape[-1]), axis=0)


def dot(a, b, dims):
    return lax.dot_general(a, b, (dims, ((), ())), preferred_element_type=F32)


def attention_kernel(
    q_ref, do_ref, k0_ref, k1_ref, k2_ref, v0_ref, v1_ref, v2_ref, cos_ref, sin_ref, bias_ref, gain_ref,
    out_ref, dq_ref, own_ref, t1_ref, t2_ref, dg_ref,
):
    rows = q_ref.shape[0]
    head = gain_ref.shape[1]
    q_gain = gain_ref[0:1, :]
    k_gain = gain_ref[1:2, :]
    cosine = cos_ref[...]
    sine = sin_ref[...]
    span = cosine.shape[0]
    q_cos = jnp.concatenate([cosine[span - rows :]] * GROUP, axis=0)
    q_sin = jnp.concatenate([sine[span - rows :]] * GROUP, axis=0)

    def stacked(ref):
        return jnp.concatenate([ref[:, j * head : (j + 1) * head] for j in range(GROUP)], axis=0)

    q_unit, q_inv = unit(stacked(q_ref).astype(F32))
    queries = rotate(q_unit * q_gain, q_cos, q_sin).astype(BF16)
    grad_out = stacked(do_ref)
    k_raw = jnp.concatenate([k2_ref[...], k1_ref[...], k0_ref[...]], axis=0).astype(F32)
    k_unit, _ = unit(k_raw)
    keys = rotate(k_unit * k_gain, cosine, sine).astype(BF16)
    values = jnp.concatenate([v2_ref[...], v1_ref[...], v0_ref[...]], axis=0)

    bias = bias_ref[...]
    scores = dot(keys, queries, ((1,), (1,))) + jnp.concatenate([bias] * GROUP, axis=1)
    d_prob = dot(values, grad_out, ((1,), (1,)))
    top = jnp.max(scores, axis=0, keepdims=True)
    exps = jnp.exp2((scores - top) * LOG2_SCALE)
    probs = exps * (1.0 / jnp.sum(exps, axis=0, keepdims=True))
    probs_b = probs.astype(BF16)
    delta = jnp.sum(probs * d_prob, axis=0, keepdims=True)
    d_score = (probs * (d_prob - delta) * SCORE_SCALE).astype(BF16)

    result = dot(probs_b, values, ((0,), (0,)))
    d_query = dot(d_score, keys, ((0,), (0,)))
    d_key = dot(d_score, queries, ((1,), (0,)))
    d_value = dot(probs_b, grad_out, ((1,), (0,)))

    far = span - rows
    t1 = d_key[far - rows : far].astype(BF16)
    t2 = d_key[: far - rows].astype(BF16)
    own_ref[0] = d_key[far:]
    own_ref[1] = d_value[far:]
    t1_ref[0] = t1
    t1_ref[1] = d_value[far - rows : far].astype(BF16)
    t2_ref[0] = t2
    t2_ref[1] = d_value[: far - rows].astype(BF16)

    d_q_y = unrotate(d_query, q_cos, q_sin)
    d_q_in = unit_back(d_q_y, q_unit, q_inv, q_gain).astype(BF16)
    for j in range(GROUP):
        out_ref[:, j * head : (j + 1) * head] = result[j * rows : (j + 1) * rows].astype(BF16)
        dq_ref[:, j * head : (j + 1) * head] = d_q_in[j * rows : (j + 1) * rows]
    d_k_terms = jnp.concatenate([t2.astype(F32), t1.astype(F32), d_key[far:]], axis=0)
    d_k_y = unrotate(d_k_terms, cosine, sine)

    @pl.when(pl.program_id(0) == 0)
    def _():
        dg_ref[...] = jnp.zeros_like(dg_ref)

    dg_ref[0:8, :] += fold(d_q_y * q_unit)
    dg_ref[8:16, :] += fold(d_k_y * k_unit)


def attention(q, d_out, ks, vs, cosine, sine, bias, gains):
    rows = q.shape[0]
    head = gains.shape[1]
    heads = ks[0].shape[1] // head
    span = cosine.shape[0]
    wide = pl.BlockSpec((rows, GROUP * head), lambda h: (0, h))
    narrow = pl.BlockSpec((rows, head), lambda h: (0, h))
    pair = pl.BlockSpec((2, rows, head), lambda h: (0, 0, h))

    def fixed(shape):
        return pl.BlockSpec(shape, lambda h: (0, 0))

    flops = 6 * 2 * heads * GROUP * rows * span * head
    return pl.pallas_call(
        attention_kernel,
        name="attention",
        grid=(heads,),
        in_specs=[wide, wide] + [narrow] * 6
        + [fixed((span, head)), fixed((span, head)), fixed((span, rows)), fixed(gains.shape)],
        out_specs=[wide, wide, pair, pair, pair, fixed((16, head))],
        out_shape=[
            jax.ShapeDtypeStruct(q.shape, BF16),
            jax.ShapeDtypeStruct(q.shape, BF16),
            jax.ShapeDtypeStruct((2, rows, heads * head), F32),
            jax.ShapeDtypeStruct((2, rows, heads * head), BF16),
            jax.ShapeDtypeStruct((2, rows, heads * head), BF16),
            jax.ShapeDtypeStruct((16, head), F32),
        ],
        cost_estimate=pl.CostEstimate(flops=flops, bytes_accessed=6_000_000, transcendentals=0),
        compiler_params=pltpu.CompilerParams(vmem_limit_bytes=32 * 1024 * 1024),
    )(q, d_out, *ks, *vs, cosine, sine, bias, gains)


def finish_kernel(own_ref, a1_ref, a2_ref, k_ref, cos_ref, sin_ref, gain_ref, dk_ref, dv_ref):
    head = gain_ref.shape[1]
    rows = k_ref.shape[0]
    span = cos_ref.shape[0]
    cosine = cos_ref[span - rows :, :]
    sine = sin_ref[span - rows :, :]
    dv_ref[...] = (own_ref[1] + a1_ref[1].astype(F32) + a2_ref[1].astype(F32)).astype(BF16)
    for j in range(k_ref.shape[1] // head):
        cols = slice(j * head, (j + 1) * head)
        d_k = own_ref[0, :, cols] + a1_ref[0, :, cols].astype(F32) + a2_ref[0, :, cols].astype(F32)
        k_unit, k_inv = unit(k_ref[:, cols].astype(F32))
        d_y = unrotate(d_k, cosine, sine)
        dk_ref[:, cols] = unit_back(d_y, k_unit, k_inv, gain_ref[1:2, :]).astype(BF16)


def finish(own, a1, a2, k, cosine, sine, gains):
    rows, width = k.shape
    head = gains.shape[1]
    step = 2 * head
    narrow = pl.BlockSpec((rows, step), lambda h: (0, h))
    pair = pl.BlockSpec((2, rows, step), lambda h: (0, 0, h))

    def fixed(shape):
        return pl.BlockSpec(shape, lambda h: (0, 0))

    return pl.pallas_call(
        finish_kernel,
        name="finish",
        grid=(width // step,),
        in_specs=[pair] * 3 + [narrow, fixed(cosine.shape), fixed(sine.shape), fixed(gains.shape)],
        out_specs=[narrow, narrow],
        out_shape=[jax.ShapeDtypeStruct(k.shape, BF16)] * 2,
        cost_estimate=pl.CostEstimate(flops=20 * rows * width, bytes_accessed=3_000_000, transcendentals=0),
        compiler_params=pltpu.CompilerParams(vmem_limit_bytes=32 * 1024 * 1024),
    )(own, a1, a2, k, cosine, sine, gains)


def all_sum(value, axis):
    count = lax.axis_size(axis)
    step = 1
    while step < count:
        value = value + lax.ppermute(value, axis, [(i, i ^ step) for i in range(count)])
        step *= 2
    return value


def on_device(q_proj, k_proj, v_proj, d_out, q_gain, k_gain):
    rows = q_proj.shape[1]
    head = q_gain.shape[0]
    blocks = WINDOW // rows
    span = WINDOW + rows
    first_row = lax.axis_index("ctx") * rows
    k1, v1 = hop(k_proj, 1), hop(v_proj, 1)
    k2, v2 = hop(k_proj, 2), hop(v_proj, 2)

    half = head // 2
    freqs = jnp.power(ROPE_BASE, -2.0 * jnp.arange(half, dtype=F32) / head)
    positions = first_row - WINDOW + jnp.arange(span, dtype=jnp.int32)
    angles = positions.astype(F32)[:, None] * freqs
    cosine = jnp.cos(angles)
    sine = jnp.sin(angles)
    cosine = jnp.concatenate([cosine, cosine], axis=1)
    sine = jnp.concatenate([-sine, sine], axis=1)
    row_ids = jnp.arange(rows, dtype=jnp.int32)[None, :]
    key_ids = jnp.arange(span, dtype=jnp.int32)[:, None]
    visible = (key_ids > row_ids) & (key_ids <= row_ids + WINDOW) & (key_ids + first_row - WINDOW >= 0)
    bias = jnp.where(visible, 0.0, HIDDEN).astype(F32)
    gains = jnp.stack([q_gain, k_gain])

    result, d_q, own, t1, t2, terms = attention(
        q_proj[0], d_out[0], (k_proj[0], k1[0], k2[0]), (v_proj[0], v1[0], v2[0]), cosine, sine, bias, gains
    )
    a1 = hop(t1, -1)
    a2 = hop(t2, -2)
    d_k, d_v = finish(own, a1, a2, k_proj[0], cosine, sine, gains)
    gain_terms = jnp.sum(terms.reshape(2, 8, head), axis=1).reshape(2 * head)
    gain_terms = all_sum(all_sum(gain_terms, "dp"), "ctx")
    share = gain_terms.shape[0] // lax.axis_size("dp")
    gain_share = lax.dynamic_slice_in_dim(gain_terms, lax.axis_index("dp") * share, share, 0)
    return (result[None], d_q[None], d_k[None], d_v[None], gain_share)


def solution(mesh):
    tokens = P("dp", "ctx", None)
    return jax.shard_map(
        on_device,
        mesh=mesh,
        in_specs=(tokens,) * 4 + (P(), P()),
        out_specs=(tokens,) * 4 + (P("dp"),),
        check_vma=False,
    )
```

time: 184 us -> 67.8 us (0.37)
  matrix products: 75.3 us -> 0 us
  local copies, waits for them, and re-layouts: 42.7 us -> 1.27 us
  blocking collectives: 24 us -> 0 us
  starting transfers between devices: 10.6 us -> 30.4 us
  other arithmetic: 18 us -> 1.12 us
  Pallas kernels: 0 us -> 16.8 us
  waiting for transfers between devices: 10.1 us -> 17.1 us
    dot_general x20 -> x0, matrix products: 65.5 us -> none  [the longest x4 20.1 us: attend(): jnp.einsum('kqe,kqd->ked', d_score, queries, preferred_element_type=jnp.f...]
    reshape x26 -> x0, local copies, waits for them, and re-layouts: 21 us -> none  [the longest x4 5.88 us: on_device(): key_grads.append(d_key.transpose(1, 0, 2).reshape(key_span, pair_width))]
    ppermute x4 -> x11, starting transfers between devices: 10.6 us -> 30.4 us  [the longest x6 16.3 us: hop(): lax.ppermute(value, 'ctx', [(i, i + steps) for i in range(initial, last)])]
    pallas_call x0 -> x2, Pallas kernels: none -> 16.8 us  [the longest x1 14.5 us: attention(): pl.pallas_call(attention_kernel, name='attention', grid=(heads,), in_spec...]
    psum x1 -> x0, blocking collectives: 14.1 us -> none  [on_device(): gathered_terms = lax.psum(gain_terms, 'ctx')]
    unnamed x1 -> x0, blocking collectives: 9.92 us -> none
    sub x4 -> x0, matrix products: 9.81 us -> none  [attend(): exponent = jnp.exp(masked - highest)]
    ppermute x4 -> x11, waiting for transfers between devices: 10.1 us -> 17.1 us  [the longest x5 15.2 us: all_sum(): lax.ppermute(value, axis, [(i, i ^ step) for i in range(count)])]
  transfers between devices with their start and end apart: 4 -> 11, of which waited for: 1 -> 6; matrix products, arithmetic and copies ran while one was open for 14% -> 3% of each run, Pallas kernels for 0% -> 0%
where the time goes in v1:
time: 67.8 us; the launch traced here: 67.5 us
  starting transfers between devices  30.4 us (45%)
  waiting for transfers between devices  17.1 us (25%)
  Pallas kernels  16.8 us (25%)
  local copies, waits for them, and re-layouts  1.27 us (2%)
  other arithmetic  1.12 us (2%)
  between operations  0.81 us (1%)
    ppermute x6, starting transfers between devices, hop(): lax.ppermute(value, 'ctx', [(i, i + steps) for i in range(initial, last)])  16.3 us
    ppermute x5, waiting for transfers between devices, all_sum(): lax.ppermute(value, axis, [(i, i ^ step) for i in range(count)])  15.2 us
    pallas_call x1, Pallas kernels, attention(): pl.pallas_call(attention_kernel, name='attention', grid=(heads,), in_spec...  14.5 us
    ppermute x5, starting transfers between devices, all_sum(): lax.ppermute(value, axis, [(i, i ^ step) for i in range(count)])  14.1 us
    pallas_call x1, Pallas kernels, finish(): pl.pallas_call(finish_kernel, name='finish', grid=(width // step,), in_sp...  2.26 us
    ppermute x6, waiting for transfers between devices, hop(): lax.ppermute(value, 'ctx', [(i, i + steps) for i in range(initial, last)])  1.98 us
  transfers between devices with their start and end apart: 11, of which 6 were waited for; matrix products, arithmetic and copies ran while one was open for 3% of the time, Pallas kernels for 0%

profile of v1, /device:TPU:0, one launch (start us, length us, event | category | flops | bytes accessed | tf_op | source)
XLA Modules:
  0.0 67.5 jit_solution(10262814766183940545)
XLA Ops:
  0.6 5.0 %collective-permute-start.1 = (bf16[1,128,1024]{2,1,0:T(8,128)(2,1)}, bf16[1,128,1024]{2,1,0:T(8,128)(2,1)S(1)}, u32[]{:S(2)}, u32[]{:S(2)}) collective-permute-start(bf16[1,128,1024]{2,1,0:T(8,128)(2,1)} %param.7), channel_id=1, source_target_pairs={{0,2},{1,3},{2,4},{3,5},{4,6},{5,7},{8,10},{9,11},{10,12},{11,13},... | collective-permute-start | bytes 786440 | tf_op jit(solution)/shard_map/ppermute | solution.py:24
  5.6 1.5 %collective-permute-start = (bf16[1,128,1024]{2,1,0:T(8,128)(2,1)}, bf16[1,128,1024]{2,1,0:T(8,128)(2,1)S(1)}, u32[]{:S(2)}, u32[]{:S(2)}) collective-permute-start(bf16[1,128,1024]{2,1,0:T(8,128)(2,1)} %param.7), channel_id=1, source_target_pairs={{0,1},{1,2},{2,3},{3,4},{4,5},{5,6},{6,7},{8,9},{9,10},{10,11},{11... | collective-permute-start | bytes 786440 | tf_op jit(solution)/shard_map/ppermute | solution.py:24
  7.1 3.9 %collective-permute-start.3 = (bf16[1,128,1024]{2,1,0:T(8,128)(2,1)}, bf16[1,128,1024]{2,1,0:T(8,128)(2,1)S(1)}, u32[]{:S(2)}, u32[]{:S(2)}) collective-permute-start(bf16[1,128,1024]{2,1,0:T(8,128)(2,1)} %param.8), channel_id=1, source_target_pairs={{0,2},{1,3},{2,4},{3,5},{4,6},{5,7},{8,10},{9,11},{10,12},{11,13},... | collective-permute-start | bytes 786440 | tf_op jit(solution)/shard_map/ppermute | solution.py:24
  11.0 3.3 %collective-permute-start.2 = (bf16[1,128,1024]{2,1,0:T(8,128)(2,1)}, bf16[1,128,1024]{2,1,0:T(8,128)(2,1)S(1)}, u32[]{:S(2)}, u32[]{:S(2)}) collective-permute-start(bf16[1,128,1024]{2,1,0:T(8,128)(2,1)} %param.8), channel_id=1, source_target_pairs={{0,1},{1,2},{2,3},{3,4},{4,5},{5,6},{6,7},{8,9},{9,10},{10,11},{11... | collective-permute-start | bytes 786440 | tf_op jit(solution)/shard_map/ppermute | solution.py:24
  14.4 0.6 copy-done.4
  15.1 0.8 %fusion.3 = (f32[384,64]{1,0:T(8,128)S(1)}, f32[384,64]{1,0:T(8,128)S(1)}, f32[384,64]{1,0:T(8,128)S(1)}) fusion(f32[64]{0:T(128)S(1)} %multiply_power_fusion, f32[384]{0:T(512)S(1)} %add_convert_fusion), kind=kLoop, calls=%fused_computation.9 | loop fusion | flops 49152 | bytes 296704 | tf_op jit(solution)/shard_map/neg | solution.py:214
  15.9 0.2 pad_maximum_fusion
  16.1 0.1 fusion.2.bias_ref
  16.2 2.0 %collective-permute-done.3 = bf16[1,128,1024]{2,1,0:T(8,128)(2,1)S(1)} collective-permute-done((bf16[1,128,1024]{2,1,0:T(8,128)(2,1)}, bf16[1,128,1024]{2,1,0:T(8,128)(2,1)S(1)}, u32[]{:S(2)}, u32[]{:S(2)}) %collective-permute-start.3) | collective-permute-done | bytes 262176 | tf_op jit(solution)/shard_map/ppermute | solution.py:24
  18.2 14.5 %attention.1 = (bf16[128,2048]{1,0:T(8,128)(2,1)}, bf16[128,2048]{1,0:T(8,128)(2,1)}, f32[2,128,1024]{2,1,0:T(8,128)S(1)}, bf16[2,128,1024]{2,1,0:T(8,128)(2,1)}...) custom-call(bf16[128,2048]{1,0:T(8,128)(2,1)S(1)} %bitcast.20, bf16[128,2048]{1,0:T(8,128)(2,1)S(1)} %bitcast.21, ...), custom_call_target="tpu_custom_call" | custom-call | flops 1207959552 | bytes 6000000 | tf_op jit(solution)/shard_map/attention/pallas_call | solution.py:132
  32.7 1.3 %collective-permute-start.4 = (bf16[2,128,1024]{2,1,0:T(8,128)(2,1)}, bf16[2,128,1024]{2,1,0:T(8,128)(2,1)S(1)}, u32[]{:S(2)}, u32[]{:S(2)}) collective-permute-start(bf16[2,128,1024]{2,1,0:T(8,128)(2,1)} %get-tuple-element.16), channel_id=1, source_target_pairs={{1,0},{2,1},{3,2},{4,3},{5,4},{6,5},{7,6},{9,8},{10,9},{11,10},{12... | collective-permute-start | bytes 1572872 | tf_op jit(solution)/shard_map/ppermute | solution.py:24
  34.0 1.3 %collective-permute-start.5 = (bf16[2,128,1024]{2,1,0:T(8,128)(2,1)S(1)}, bf16[2,128,1024]{2,1,0:T(8,128)(2,1)S(1)}, u32[]{:S(2)}, u32[]{:S(2)}) collective-permute-start(bf16[2,128,1024]{2,1,0:T(8,128)(2,1)S(1)} %get-tuple-element.17), channel_id=1, source_target_pairs={{2,0},{3,1},{4,2},{5,3},{6,4},{7,5},{10,8},{11,9},{12,10},{13,11},... | collective-permute-start | bytes 1572872 | tf_op jit(solution)/shard_map/ppermute | solution.py:24
  35.3 1.6 %collective-permute-start.6 = (f32[256]{0:T(256)S(1)}, f32[256]{0:T(256)S(1)}, u32[]{:S(2)}, u32[]{:S(2)}) collective-permute-start(f32[256]{0:T(256)S(1)} %bitcast.27), channel_id=1, source_target_pairs={{0,8},{8,0},{16,24},{24,16},{1,9},{9,1},{17,25},{25,17},{2,10},{10... | collective-permute-start | bytes 3080 | tf_op jit(solution)/shard_map/ppermute | solution.py:193
  36.9 2.1 %collective-permute-done.6 = f32[256]{0:T(256)S(1)} collective-permute-done((f32[256]{0:T(256)S(1)}, f32[256]{0:T(256)S(1)}, u32[]{:S(2)}, u32[]{:S(2)}) %collective-permute-start.6) | collective-permute-done | bytes 1056 | tf_op jit(solution)/shard_map/ppermute | solution.py:193
  39.0 1.5 %collective-permute-start.7 = (f32[256]{0:T(256)S(1)}, f32[256]{0:T(256)S(1)}, u32[]{:S(2)}, u32[]{:S(2)}) collective-permute-start(f32[256]{0:T(256)S(1)} %bitcast_add_fusion), channel_id=1, source_target_pairs={{0,16},{8,24},{16,0},{24,8},{1,17},{9,25},{17,1},{25,9},{2,18},{10... | collective-permute-start | bytes 3080 | tf_op jit(solution)/shard_map/ppermute | solution.py:193
  40.5 2.1 %collective-permute-done.7 = f32[256]{0:T(256)S(1)} collective-permute-done((f32[256]{0:T(256)S(1)}, f32[256]{0:T(256)S(1)}, u32[]{:S(2)}, u32[]{:S(2)}) %collective-permute-start.7) | collective-permute-done | bytes 1056 | tf_op jit(solution)/shard_map/ppermute | solution.py:193
  42.6 2.9 %collective-permute-start.8 = (f32[256]{0:T(256)S(1)}, f32[256]{0:T(256)S(1)}, u32[]{:S(2)}, u32[]{:S(2)}) collective-permute-start(f32[256]{0:T(256)S(1)} %add.64), channel_id=1, source_target_pairs={{0,1},{1,0},{2,3},{3,2},{4,5},{5,4},{6,7},{7,6},{8,9},{9,8},{10,11... | collective-permute-start | bytes 3080 | tf_op jit(solution)/shard_map/ppermute | solution.py:193
  45.5 0.8 %collective-permute-done.8 = f32[256]{0:T(256)S(1)} collective-permute-done((f32[256]{0:T(256)S(1)}, f32[256]{0:T(256)S(1)}, u32[]{:S(2)}, u32[]{:S(2)}) %collective-permute-start.8) | collective-permute-done | bytes 1056 | tf_op jit(solution)/shard_map/ppermute | solution.py:193
  46.3 5.5 %collective-permute-start.9 = (f32[256]{0:T(256)S(1)}, f32[256]{0:T(256)S(1)}, u32[]{:S(2)}, u32[]{:S(2)}) collective-permute-start(f32[256]{0:T(256)S(1)} %add.65), channel_id=1, source_target_pairs={{0,2},{1,3},{2,0},{3,1},{4,6},{5,7},{6,4},{7,5},{8,10},{9,11},{10,... | collective-permute-start | bytes 3080 | tf_op jit(solution)/shard_map/ppermute | solution.py:193
  51.9 8.3 %collective-permute-done.9 = f32[256]{0:T(256)S(1)} collective-permute-done((f32[256]{0:T(256)S(1)}, f32[256]{0:T(256)S(1)}, u32[]{:S(2)}, u32[]{:S(2)}) %collective-permute-start.9) | collective-permute-done | bytes 1056 | tf_op jit(solution)/shard_map/ppermute | solution.py:193
  60.2 2.6 %collective-permute-start.10 = (f32[256]{0:T(256)S(1)}, f32[256]{0:T(256)S(1)}, u32[]{:S(2)}, u32[]{:S(2)}) collective-permute-start(f32[256]{0:T(256)S(1)} %add.66), channel_id=1, source_target_pairs={{0,4},{1,5},{2,6},{3,7},{4,0},{5,1},{6,2},{7,3},{8,12},{9,13},{10,... | collective-permute-start | bytes 3080 | tf_op jit(solution)/shard_map/ppermute | solution.py:193
  62.8 1.9 %collective-permute-done.10 = f32[256]{0:T(256)S(1)} collective-permute-done((f32[256]{0:T(256)S(1)}, f32[256]{0:T(256)S(1)}, u32[]{:S(2)}, u32[]{:S(2)}) %collective-permute-start.10) | collective-permute-done | bytes 1056 | tf_op jit(solution)/shard_map/ppermute | solution.py:193
  64.7 0.6 dynamic_slice.3
  65.2 2.3 %finish.1 = (bf16[128,1024]{1,0:T(8,128)(2,1)}, bf16[128,1024]{1,0:T(8,128)(2,1)}) custom-call(f32[2,128,1024]{2,1,0:T(8,128)S(1)} %get-tuple-element.15.own_ref, bf16[2,128,1024]{2,1,0:T(8,128)(2,1)S(1)} %collective-permute-done.4.a1_ref, bf16[2,128,1024]{2,1,0:T(8,128)(2,1)S(1)} %collective-permute-done.5.a2_ref, bf16[128,1024]{1,0:T(8,128)(2,1)S(1)} %bitcast.19, ...), custom_call_target="tpu_custom_call" | custom-call | flops 2621440 | bytes 3000000 | tf_op jit(solution)/shard_map/finish/pallas_call | solution.py:177
  (27 shorter events, 0.1 us)
Async XLA Ops:
  0.6 15.6 %collective-permute-start.1 = (bf16[1,128,1024]{2,1,0:T(8,128)(2,1)}, bf16[1,128,1024]{2,1,0:T(8,128)(2,1)S(1)}, u32[]{:S(2)}, u32[]{:S(2)}) collective-permute-start(bf16[1,128,1024]{2,1,0:T(8,128)(2,1)} %param.7), channel_id=1, source_target_pairs={{0,2},{1,3},{2,4},{3,5},{4,6},{5,7},{8,10},{9,11},{10,12},{11,13},... | collective-permute-start | bytes 786440 | tf_op jit(solution)/shard_map/ppermute | solution.py:24
  5.6 10.6 %collective-permute-start = (bf16[1,128,1024]{2,1,0:T(8,128)(2,1)}, bf16[1,128,1024]{2,1,0:T(8,128)(2,1)S(1)}, u32[]{:S(2)}, u32[]{:S(2)}) collective-permute-start(bf16[1,128,1024]{2,1,0:T(8,128)(2,1)} %param.7), channel_id=1, source_target_pairs={{0,1},{1,2},{2,3},{3,4},{4,5},{5,6},{6,7},{8,9},{9,10},{10,11},{11... | collective-permute-start | bytes 786440 | tf_op jit(solution)/shard_map/ppermute | solution.py:24
  7.1 11.1 %collective-permute-start.3 = (bf16[1,128,1024]{2,1,0:T(8,128)(2,1)}, bf16[1,128,1024]{2,1,0:T(8,128)(2,1)S(1)}, u32[]{:S(2)}, u32[]{:S(2)}) collective-permute-start(bf16[1,128,1024]{2,1,0:T(8,128)(2,1)} %param.8), channel_id=1, source_target_pairs={{0,2},{1,3},{2,4},{3,5},{4,6},{5,7},{8,10},{9,11},{10,12},{11,13},... | collective-permute-start | bytes 786440 | tf_op jit(solution)/shard_map/ppermute | solution.py:24
  11.0 7.2 %collective-permute-start.2 = (bf16[1,128,1024]{2,1,0:T(8,128)(2,1)}, bf16[1,128,1024]{2,1,0:T(8,128)(2,1)S(1)}, u32[]{:S(2)}, u32[]{:S(2)}) collective-permute-start(bf16[1,128,1024]{2,1,0:T(8,128)(2,1)} %param.8), channel_id=1, source_target_pairs={{0,1},{1,2},{2,3},{3,4},{4,5},{5,6},{6,7},{8,9},{9,10},{10,11},{11... | collective-permute-start | bytes 786440 | tf_op jit(solution)/shard_map/ppermute | solution.py:24
  14.4 0.7 copy-start.4
  14.4 0.7 copy-start.5
  15.1 3.1 %copy-start.2 = (bf16[1,128,2048]{2,1,0:T(8,128)(2,1)S(1)}, bf16[1,128,2048]{2,1,0:T(8,128)(2,1)}, u32[]{:S(2)}) copy-start(bf16[1,128,2048]{2,1,0:T(8,128)(2,1)} %param.9) | copy-start | bytes 1572868
  15.9 2.3 %copy-start = (bf16[1,128,1024]{2,1,0:T(8,128)(2,1)S(1)}, bf16[1,128,1024]{2,1,0:T(8,128)(2,1)}, u32[]{:S(2)}) copy-start(bf16[1,128,1024]{2,1,0:T(8,128)(2,1)} %param.7) | copy-start | bytes 786436
  15.9 2.3 %copy-start.1 = (bf16[1,128,2048]{2,1,0:T(8,128)(2,1)S(1)}, bf16[1,128,2048]{2,1,0:T(8,128)(2,1)}, u32[]{:S(2)}) copy-start(bf16[1,128,2048]{2,1,0:T(8,128)(2,1)} %param.6) | copy-start | bytes 1572868
  15.9 2.3 %copy-start.3 = (bf16[1,128,1024]{2,1,0:T(8,128)(2,1)S(1)}, bf16[1,128,1024]{2,1,0:T(8,128)(2,1)}, u32[]{:S(2)}) copy-start(bf16[1,128,1024]{2,1,0:T(8,128)(2,1)} %param.8) | copy-start | bytes 786436
  32.7 32.5 %collective-permute-start.4 = (bf16[2,128,1024]{2,1,0:T(8,128)(2,1)}, bf16[2,128,1024]{2,1,0:T(8,128)(2,1)S(1)}, u32[]{:S(2)}, u32[]{:S(2)}) collective-permute-start(bf16[2,128,1024]{2,1,0:T(8,128)(2,1)} %get-tuple-element.16), channel_id=1, source_target_pairs={{1,0},{2,1},{3,2},{4,3},{5,4},{6,5},{7,6},{9,8},{10,9},{11,10},{12... | collective-permute-start | bytes 1572872 | tf_op jit(solution)/shard_map/ppermute | solution.py:24
  34.0 31.2 %collective-permute-start.5 = (bf16[2,128,1024]{2,1,0:T(8,128)(2,1)S(1)}, bf16[2,128,1024]{2,1,0:T(8,128)(2,1)S(1)}, u32[]{:S(2)}, u32[]{:S(2)}) collective-permute-start(bf16[2,128,1024]{2,1,0:T(8,128)(2,1)S(1)} %get-tuple-element.17), channel_id=1, source_target_pairs={{2,0},{3,1},{4,2},{5,3},{6,4},{7,5},{10,8},{11,9},{12,10},{13,11},... | collective-permute-start | bytes 1572872 | tf_op jit(solution)/shard_map/ppermute | solution.py:24
  35.3 3.6 %collective-permute-start.6 = (f32[256]{0:T(256)S(1)}, f32[256]{0:T(256)S(1)}, u32[]{:S(2)}, u32[]{:S(2)}) collective-permute-start(f32[256]{0:T(256)S(1)} %bitcast.27), channel_id=1, source_target_pairs={{0,8},{8,0},{16,24},{24,16},{1,9},{9,1},{17,25},{25,17},{2,10},{10... | collective-permute-start | bytes 3080 | tf_op jit(solution)/shard_map/ppermute | solution.py:193
  39.0 3.6 %collective-permute-start.7 = (f32[256]{0:T(256)S(1)}, f32[256]{0:T(256)S(1)}, u32[]{:S(2)}, u32[]{:S(2)}) collective-permute-start(f32[256]{0:T(256)S(1)} %bitcast_add_fusion), channel_id=1, source_target_pairs={{0,16},{8,24},{16,0},{24,8},{1,17},{9,25},{17,1},{25,9},{2,18},{10... | collective-permute-start | bytes 3080 | tf_op jit(solution)/shard_map/ppermute | solution.py:193
  42.6 3.7 %collective-permute-start.8 = (f32[256]{0:T(256)S(1)}, f32[256]{0:T(256)S(1)}, u32[]{:S(2)}, u32[]{:S(2)}) collective-permute-start(f32[256]{0:T(256)S(1)} %add.64), channel_id=1, source_target_pairs={{0,1},{1,0},{2,3},{3,2},{4,5},{5,4},{6,7},{7,6},{8,9},{9,8},{10,11... | collective-permute-start | bytes 3080 | tf_op jit(solution)/shard_map/ppermute | solution.py:193
  46.3 13.9 %collective-permute-start.9 = (f32[256]{0:T(256)S(1)}, f32[256]{0:T(256)S(1)}, u32[]{:S(2)}, u32[]{:S(2)}) collective-permute-start(f32[256]{0:T(256)S(1)} %add.65), channel_id=1, source_target_pairs={{0,2},{1,3},{2,0},{3,1},{4,6},{5,7},{6,4},{7,5},{8,10},{9,11},{10,... | collective-permute-start | bytes 3080 | tf_op jit(solution)/shard_map/ppermute | solution.py:193
  60.2 4.5 %collective-permute-start.10 = (f32[256]{0:T(256)S(1)}, f32[256]{0:T(256)S(1)}, u32[]{:S(2)}, u32[]{:S(2)}) collective-permute-start(f32[256]{0:T(256)S(1)} %add.66), channel_id=1, source_target_pairs={{0,4},{1,5},{2,6},{3,7},{4,0},{5,1},{6,2},{7,3},{8,12},{9,13},{10,... | collective-permute-start | bytes 3080 | tf_op jit(solution)/shard_map/ppermute | solution.py:193

commit v2 on v1

v2 whole, which is shorter than its diff:
```python
import math

import jax
import jax.numpy as jnp
from jax import lax
from jax.experimental import pallas as pl
from jax.experimental.pallas import tpu as pltpu
from jax.sharding import PartitionSpec as P

WINDOW = 256
EPSILON = 1e-06
ROPE_BASE = 10000.0
SCORE_SCALE = 168.0 ** (-0.5)
LOG2_SCALE = SCORE_SCALE * math.log2(math.e)
HIDDEN = -1e30
GROUP = 2
F32 = jnp.float32
BF16 = jnp.bfloat16
UNROLL = 8
TABLES_COST = 10_000_000_000
IN_VMEM = pl.BlockSpec(memory_space=pltpu.VMEM)
VMEM_LIMIT = 24 * 1024 * 1024


def hop(value, steps):
    count = lax.axis_size("ctx")
    initial, last = (max(0, -steps), min(count, count - steps))
    return lax.ppermute(value, "ctx", [(i, i + steps) for i in range(initial, last)])


def ring_hop(value, steps):
    count = lax.axis_size("ctx")
    return lax.ppermute(value, "ctx", [(i, (i + steps) % count) for i in range(count)])


def swap_pairs(value):
    return lax.ppermute(value, "ctx", [(i, i ^ 1) for i in range(lax.axis_size("ctx"))])


def dot(a, b, dims=((1,), (0,))):
    return lax.dot_general(a, b, (dims, ((), ())), preferred_element_type=F32)


def swap_matrix(head):
    rows = lax.broadcasted_iota(jnp.int32, (head, head), 0)
    cols = lax.broadcasted_iota(jnp.int32, (head, head), 1)
    return jnp.where(jnp.abs(rows - cols) == head // 2, 1.0, 0.0).astype(BF16)


def row_mean(x):
    head = x.shape[-1]
    high = x.astype(BF16)
    low = (x - high.astype(F32)).astype(BF16)
    return dot(jnp.concatenate([high, low], axis=1), jnp.full((2 * head, head), 1.0 / head, BF16))


def norm_rotate(x_b, turn, turn_swapped, swap):
    x = x_b.astype(F32)
    inverse = lax.rsqrt(row_mean(x * x) + EPSILON)
    rotated = (inverse * (x * turn + dot(x_b, swap) * turn_swapped)).astype(BF16)
    return rotated, dot(rotated, swap).astype(BF16), x * inverse, inverse


def norm_back(d_y, normed, inverse, gain):
    d_normed = d_y * gain
    return inverse * (d_normed - normed * row_mean(d_normed * normed))


def fold(x):
    return jnp.sum(x.reshape(-1, 8, x.shape[-1]), axis=0)


def columns(index, size):
    return pl.ds(pl.multiple_of(index * size, size), size)


def stacked(ref, h, head):
    return jnp.concatenate([ref[:, columns(GROUP * h + j, head)] for j in range(GROUP)], axis=0)


def each_head(count, body):
    def several(i, carry):
        for u in range(UNROLL):
            body(i * UNROLL + u)
        return carry

    lax.fori_loop(0, count // UNROLL, several, 0)


def call(kernel, name, outs, args, flops=1_000_000, traffic=100_000, scratch=()):
    return pl.pallas_call(
        kernel,
        name=name,
        in_specs=[IN_VMEM] * len(args),
        out_specs=[IN_VMEM] * len(outs),
        out_shape=[jax.ShapeDtypeStruct(shape, dtype) for shape, dtype in outs],
        scratch_shapes=scratch,
        cost_estimate=pl.CostEstimate(flops=flops, bytes_accessed=traffic, transcendentals=0),
        compiler_params=pltpu.CompilerParams(vmem_limit_bytes=VMEM_LIMIT),
    )(*args)


def tables_kernel(freq_ref, angle_ref):
    span, head = angle_ref.shape[1:]
    rows = span - WINDOW
    position = lax.axis_index("ctx") * rows - WINDOW + lax.broadcasted_iota(jnp.int32, (span, head), 0)
    angles = position.astype(F32) * freq_ref[0:1]
    angle_ref[0] = jnp.cos(angles)
    angle_ref[1] = jnp.sin(angles) * freq_ref[1:2]


def prepare_kernel(
    q_ref, k_ref, q_gain_ref, k_gain_ref, angle_ref,
    q_ref2, q_unit_ref, q_inv_ref, k_ref2, k_unit_ref, k_inv_ref, turn_ref,
):
    heads, group_rows, head = q_unit_ref.shape
    rows = group_rows // GROUP
    half = head // 2
    swap = swap_matrix(head)
    span = angle_ref.shape[1]
    far = span - rows
    cosine, sine = angle_ref[0], angle_ref[1]
    q_gain, k_gain = q_gain_ref[...], k_gain_ref[...]
    q_turn = jnp.concatenate([cosine[far:] * q_gain] * GROUP, axis=0)
    q_turn_s = jnp.concatenate([sine[far:] * pltpu.roll(q_gain, half, 1)] * GROUP, axis=0)
    k_turn_all = cosine * k_gain
    k_turn_all_s = sine * pltpu.roll(k_gain, half, 1)
    turn_ref[0] = k_turn_all[:far]
    turn_ref[1] = k_turn_all_s[:far]
    k_turn, k_turn_s = k_turn_all[far:], k_turn_all_s[far:]

    def body(h):
        rotated, swapped, normed, inverse = norm_rotate(stacked(q_ref, h, head), q_turn, q_turn_s, swap)
        q_ref2[h, :, :head] = rotated
        q_ref2[h, :, head:] = swapped
        q_unit_ref[h] = normed
        q_inv_ref[h] = inverse
        rotated, swapped, normed, inverse = norm_rotate(k_ref[:, columns(h, head)], k_turn, k_turn_s, swap)
        k_ref2[h, :, :head] = rotated
        k_ref2[h, :, head:] = swapped
        k_unit_ref[h] = normed
        k_inv_ref[h] = inverse

    each_head(heads, body)


def scores_kernel(
    q_ref, do_ref, own_ref, k1a_ref, k1b_ref, k2_ref, turn_ref,
    probs_ref, keys_ref, unit_ref, dv_ref, dv1_ref, dv2_ref,
):
    heads, span, _ = probs_ref.shape
    rows, head = own_ref.shape[1], own_ref.shape[2] // 2
    far = span - rows
    odd = lax.rem(lax.axis_index("ctx"), 2) == 1
    swap = swap_matrix(head)
    turn, turn_s = turn_ref[0], turn_ref[1]
    key = lax.broadcasted_iota(jnp.int32, (span, rows), 0)
    row = lax.broadcasted_iota(jnp.int32, (span, rows), 1)
    start = far - lax.axis_index("ctx") * rows
    bias = jnp.where((key > row) & (key <= row + far) & (key >= start), 0.0, HIDDEN)
    bias = jnp.concatenate([bias] * GROUP, axis=1)

    def body(h):
        cols = columns(h, head)
        raw = jnp.concatenate([k2_ref[:, cols], jnp.where(odd, k1a_ref[:, cols], k1b_ref[:, cols])], axis=0)
        rotated, swapped, normed, _ = norm_rotate(raw, turn, turn_s, swap)
        keys_ref[h, :, :head] = rotated
        keys_ref[h, :, head:] = swapped
        unit_ref[h] = normed
        keys = jnp.concatenate([rotated, own_ref[h, :, :head]], axis=0)
        scores = dot(keys, q_ref[h, :, :head], ((1,), (1,))) + bias
        top = jnp.max(scores, axis=0, keepdims=True)
        exps = jnp.exp2((scores - top) * LOG2_SCALE)
        probs = exps * (1.0 / jnp.sum(exps, axis=0, keepdims=True))
        probs_ref[h] = probs
        d_value = dot(probs.astype(BF16), stacked(do_ref, h, head))
        dv2_ref[:, cols] = d_value[: far - rows].astype(BF16)
        dv1_ref[:, cols] = d_value[far - rows : far].astype(BF16)
        dv_ref[:, cols] = d_value[far:]

    each_head(heads, body)


def grads_kernel(
    probs_ref, q_ref, q_unit_ref, do_ref, keys_ref, own_ref, unit_ref, own_unit_ref, v0_ref, v1a_ref, v1b_ref, v2_ref,
    angle_ref,
    dqy_ref, dy_ref, dk1_ref, dk2_ref, sum_ref, dg_ref,
):
    heads, span, _ = probs_ref.shape
    rows, head = own_ref.shape[1], own_ref.shape[2] // 2
    far = span - rows
    odd = lax.rem(lax.axis_index("ctx"), 2) == 1
    cosine, sine = angle_ref[0], angle_ref[1]
    q_cos = jnp.concatenate([cosine[far:]] * GROUP, axis=0)
    q_sin = jnp.concatenate([sine[far:]] * GROUP, axis=0)
    dg_ref[...] = jnp.zeros_like(dg_ref)

    def body(h):
        cols = columns(h, head)
        values = jnp.concatenate([v2_ref[:, cols], jnp.where(odd, v1a_ref[:, cols], v1b_ref[:, cols]), v0_ref[:, cols]], axis=0)
        grad_out = stacked(do_ref, h, head)
        probs = probs_ref[h]
        d_prob = dot(values, grad_out, ((1,), (1,)))
        delta = jnp.sum(probs * d_prob, axis=0, keepdims=True)
        d_score = (probs * (d_prob - delta) * SCORE_SCALE).astype(BF16)
        d_key = dot(d_score, q_ref[h])
        d_query = dot(d_score, jnp.concatenate([keys_ref[h], own_ref[h]], axis=0), ((0,), (0,)))

        dk2_ref[:, cols] = d_key[: far - rows, :head].astype(BF16)
        dk1_ref[:, cols] = d_key[far - rows : far, :head].astype(BF16)
        term = d_key[:far].astype(BF16).astype(F32)
        d_y_far = term[:, :head] * cosine[:far] - term[:, head:] * sine[:far]
        d_y_own = d_key[far:, :head] * cosine[far:] - d_key[far:, head:] * sine[far:]
        dy_ref[:, cols] = d_y_own
        dg_ref[8:16, :] += fold(d_y_far * unit_ref[h]) + fold(d_y_own * own_unit_ref[h])

        d_y = d_query[:, :head] * q_cos - d_query[:, head:] * q_sin
        dqy_ref[h] = d_y
        dg_ref[0:8, :] += fold(d_y * q_unit_ref[h])

    each_head(heads, body)
    sum_ref[0:1] = jnp.sum(dg_ref[0:8], axis=0, keepdims=True)
    sum_ref[1:2] = jnp.sum(dg_ref[8:16], axis=0, keepdims=True)


def outputs_kernel(probs_ref, v0_ref, v1a_ref, v1b_ref, v2_ref, dqy_ref, q_unit_ref, q_inv_ref, gain_ref, out_ref, dq_ref):
    heads, group_rows, head = q_unit_ref.shape
    rows = group_rows // GROUP
    odd = lax.rem(lax.axis_index("ctx"), 2) == 1
    q_gain = gain_ref[...]

    def body(h):
        cols = columns(h, head)
        values = jnp.concatenate([v2_ref[:, cols], jnp.where(odd, v1a_ref[:, cols], v1b_ref[:, cols]), v0_ref[:, cols]], axis=0)
        result = dot(probs_ref[h].astype(BF16), values, ((0,), (0,))).astype(BF16)
        d_q = norm_back(dqy_ref[h], q_unit_ref[h], q_inv_ref[h], q_gain).astype(BF16)
        for j in range(GROUP):
            wide = columns(GROUP * h + j, head)
            out_ref[:, wide] = result[j * rows : (j + 1) * rows]
            dq_ref[:, wide] = d_q[j * rows : (j + 1) * rows]

    each_head(heads, body)


def merge_kernel(k_far_ref, k_near_ref, v_far_ref, v_near_ref, out_ref):
    odd = lax.rem(lax.axis_index("ctx"), 2) == 1
    for i, (far_ref, near_ref) in enumerate(((k_far_ref, k_near_ref), (v_far_ref, v_near_ref))):
        near = jnp.where(odd, near_ref[...].astype(F32), 0.0)
        out_ref[i] = (far_ref[...].astype(F32) + near).astype(BF16)


def finish_kernel(dy_ref, dv_ref, k1_ref, v1_ref, far_ref, unit_ref, inv_ref, angle_ref, gain_ref, dk_out, dv_out):
    heads, rows, head = unit_ref.shape
    far = angle_ref.shape[1] - rows
    odd = lax.rem(lax.axis_index("ctx"), 2) == 1
    swap = swap_matrix(head)
    swaps = jnp.concatenate([swap, swap], axis=0)
    cosine, sine = angle_ref[0, far:], angle_ref[1, far:]
    gain = gain_ref[...]

    def body(h):
        cols = columns(h, head)
        near = jnp.where(odd, 0.0, v1_ref[:, cols].astype(F32))
        dv_out[:, cols] = (dv_ref[:, cols] + near + far_ref[1, :, cols].astype(F32)).astype(BF16)
        near = jnp.where(odd, 0.0, k1_ref[:, cols].astype(F32))
        rest = far_ref[0, :, cols]
        swapped = dot(jnp.concatenate([near.astype(BF16), rest], axis=1), swaps)
        d_y = dy_ref[:, cols] + ((near + rest.astype(F32)) * cosine - swapped * sine)
        dk_out[:, cols] = norm_back(d_y, unit_ref[h], inv_ref[h], gain).astype(BF16)

    each_head(heads, body)


def share_kernel(own_ref, other_ref, out_ref):
    total = own_ref[...] + other_ref[...]
    head, size = total.shape[1], out_ref.shape[1]
    share = jnp.zeros(out_ref.shape, F32)
    for j in range(total.size // size):
        row, col = divmod(j * size, head)
        share = jnp.where(lax.axis_index("dp") == j, total[row : row + 1, col : col + size], share)
    out_ref[...] = share


def all_sum_term(value, axis, step):
    return lax.ppermute(value, axis, [(i, i ^ step) for i in range(lax.axis_size(axis))])


def all_sum(value, axis, steps):
    for step in steps:
        value = value + all_sum_term(value, axis, step)
    return value


def doublings(axis, first=1):
    count = lax.axis_size(axis)
    return [first << i for i in range(count.bit_length()) if first << i < count]


def on_device(q_proj, k_proj, v_proj, d_out, q_gain, k_gain):
    rows = q_proj.shape[1]
    head = q_gain.shape[0]
    heads = k_proj.shape[2] // head
    width = heads * head
    wide = GROUP * width
    span = WINDOW + rows
    far = WINDOW
    assert far == 2 * rows
    tall = GROUP * rows
    k2 = hop(k_proj, 2)
    v2 = ring_hop(v_proj, 2)
    k1_odd = swap_pairs(k_proj)
    v1_odd = swap_pairs(v_proj)

    half = head // 2
    freqs = jnp.power(ROPE_BASE, -2.0 * jnp.arange(half, dtype=F32) / head)
    sign = jnp.where(jnp.arange(head) < half, -1.0, 1.0)
    freqs = jnp.stack([jnp.tile(freqs, 2), sign])

    q_gain = q_gain.reshape(1, head)
    k_gain = k_gain.reshape(1, head)
    (angle_table,) = call(tables_kernel, "tables", [((2, span, head), F32)], (freqs,), flops=TABLES_COST)
    q_rot, q_unit, q_inv, k_rot, k_unit, k_inv, turn_table = call(
        prepare_kernel,
        "prepare",
        [((heads, tall, 2 * head), BF16), ((heads, tall, head), F32), ((heads, tall, head), F32)]
        + [((heads, rows, 2 * head), BF16), ((heads, rows, head), F32), ((heads, rows, head), F32)]
        + [((2, far, head), F32)],
        (q_proj[0], k_proj[0], q_gain, k_gain, angle_table),
    )
    q_rot, k2 = lax.optimization_barrier((q_rot, k2))
    k1_even, v2 = lax.optimization_barrier((swap_pairs(k2), v2))
    k1 = k1_odd[0], k1_even[0]
    v1 = v1_odd[0], swap_pairs(v2)[0]
    probs, far_keys, far_unit, dv_own, dv1, dv2 = call(
        scores_kernel,
        "scores",
        [((heads, span, tall), F32), ((heads, far, 2 * head), BF16), ((heads, far, head), F32)]
        + [((rows, width), F32), ((rows, width), BF16), ((rows, width), BF16)],
        (q_rot, d_out[0], k_rot, *k1, k2[0], turn_table),
    )
    dv_near = swap_pairs(dv1)
    dq_y, dy_own, dk1, dk2, gain_terms = call(
        grads_kernel,
        "grads",
        [((heads, tall, head), F32), ((rows, width), F32), ((rows, width), BF16), ((rows, width), BF16)]
        + [((2, head), F32)],
        (probs, q_rot, q_unit, d_out[0], far_keys, k_rot, far_unit, k_unit, v_proj[0], *v1, v2[0], angle_table),
        scratch=[pltpu.VMEM((16, head), F32)],
    )
    dk_near = swap_pairs(dk1)
    gain_terms = all_sum(gain_terms, "ctx", [2])
    gain_terms, dk_near = lax.optimization_barrier((gain_terms, dk_near))
    (merged,) = call(merge_kernel, "merge", [((2, rows, width), BF16)], (dk2, dk_near, dv2, dv_near))
    back = hop(merged, -2)
    gain_terms = all_sum(all_sum(gain_terms, "dp", doublings("dp")), "ctx", [1])
    result, d_q = call(
        outputs_kernel,
        "outputs",
        [((rows, wide), BF16), ((rows, wide), BF16)],
        (probs, v_proj[0], *v1, v2[0], dq_y, q_unit, q_inv, q_gain),
    )
    gain_terms, back, result, d_q = lax.optimization_barrier((gain_terms, back, result, d_q))
    for step in doublings("ctx", 4)[:-1]:
        gain_terms = all_sum(gain_terms, "ctx", [step])
    last = doublings("ctx", 4)[-1]
    others = all_sum_term(gain_terms, "ctx", last)
    d_k, d_v = call(
        finish_kernel,
        "finish",
        [((rows, width), BF16), ((rows, width), BF16)],
        (dy_own, dv_own, dk_near, dv_near, back, k_unit, k_inv, angle_table, k_gain),
    )
    share = 2 * head // lax.axis_size("dp")
    (gain_share,) = call(share_kernel, "share", [((1, share), F32)], (gain_terms, others))
    return (result[None], d_q[None], d_k[None], d_v[None], gain_share[0])


def solution(mesh):
    tokens = P("dp", "ctx", None)
    return jax.shard_map(
        on_device,
        mesh=mesh,
        in_specs=(tokens,) * 4 + (P(), P()),
        out_specs=(tokens,) * 4 + (P("dp"),),
        check_vma=False,
    )
```

time: 67.8 us -> 50.5 us (0.74)
  starting transfers between devices: 30.4 us -> 17.2 us
  Pallas kernels: 16.8 us -> 15.6 us
  other arithmetic: 1.12 us -> 0.04 us
  local copies, waits for them, and re-layouts: 1.27 us -> 0.41 us
  waiting for transfers between devices: 17.1 us -> 16.3 us
    ppermute x6 -> x2, starting transfers between devices: 16.3 us -> 6.27 us  [hop(): lax.ppermute(value, 'ctx', [(i, i + steps) for i in range(initial, last)])]
    ppermute x5 -> x12, waiting for transfers between devices: 15.2 us -> 9.98 us  [the longest x5 6 us: all_sum_term(): lax.ppermute(value, axis, [(i, i ^ step) for i in range(lax.axis_size(axi...]
    ppermute x6 -> x2, waiting for transfers between devices: 1.98 us -> 6.3 us  [hop(): lax.ppermute(value, 'ctx', [(i, i + steps) for i in range(initial, last)])]
    ppermute x5 -> x12, starting transfers between devices: 14.1 us -> 11 us  [the longest x5 8.2 us: all_sum_term(): lax.ppermute(value, axis, [(i, i ^ step) for i in range(lax.axis_size(axi...]
    pallas_call x2 -> x8, Pallas kernels: 16.8 us -> 15.6 us  [call(): pl.pallas_call(kernel, name=name, in_specs=[IN_VMEM] * len(args), out_spe...]
    neg x1 -> x0, other arithmetic: 0.76 us -> none  [on_device(): sine = jnp.concatenate([-sine, sine], axis=1)]
  transfers between devices with their start and end apart: 11 -> 14, of which waited for: 6 -> 7; matrix products, arithmetic and copies ran while one was open for 3% -> 0% of each run, Pallas kernels for 0% -> 23%
where the time goes in v2:
time: 50.5 us; the launch traced here: 50.3 us
  starting transfers between devices  17.2 us (34%)
  waiting for transfers between devices  16.3 us (32%)
  Pallas kernels  15.6 us (31%)
  between operations  0.77 us (2%)
    pallas_call x8, Pallas kernels, call(): pl.pallas_call(kernel, name=name, in_specs=[IN_VMEM] * len(args), out_spe...  15.6 us
    ppermute x5, starting transfers between devices, all_sum_term(): lax.ppermute(value, axis, [(i, i ^ step) for i in range(lax.axis_size(axi...  8.2 us
    ppermute x2, waiting for transfers between devices, hop(): lax.ppermute(value, 'ctx', [(i, i + steps) for i in range(initial, last)])  6.3 us
    ppermute x2, starting transfers between devices, hop(): lax.ppermute(value, 'ctx', [(i, i + steps) for i in range(initial, last)])  6.27 us
    ppermute x5, waiting for transfers between devices, all_sum_term(): lax.ppermute(value, axis, [(i, i ^ step) for i in range(lax.axis_size(axi...  6 us
    ppermute x1, waiting for transfers between devices, ring_hop(): lax.ppermute(value, 'ctx', [(i, (i + steps) % count) for i in range(count)])  3.97 us
    ppermute x1, starting transfers between devices, ring_hop(): lax.ppermute(value, 'ctx', [(i, (i + steps) % count) for i in range(count)])  1.62 us
    ppermute x6, starting transfers between devices, swap_pairs(): lax.ppermute(value, 'ctx', [(i, i ^ 1) for i in range(lax.axis_size('ctx'...  1.16 us
  transfers between devices with their start and end apart: 14, of which 7 were waited for; matrix products, arithmetic and copies ran while one was open for 0% of the time, Pallas kernels for 23%

profile of v2, /device:TPU:0, one launch (start us, length us, event | category | flops | bytes accessed | tf_op | source)
XLA Modules:
  0.0 50.3 jit_solution(16202125005589805359)
XLA Ops:
  0.6 5.0 %collective-permute-start = (bf16[1,128,1024]{2,1,0:T(8,128)(2,1)}, bf16[1,128,1024]{2,1,0:T(8,128)(2,1)S(1)}, u32[]{:S(2)}, u32[]{:S(2)}) collective-permute-start(bf16[1,128,1024]{2,1,0:T(8,128)(2,1)} %param.7), channel_id=1, source_target_pairs={{0,2},{1,3},{2,4},{3,5},{4,6},{5,7},{8,10},{9,11},{10,12},{11,13},... | collective-permute-start | bytes 786440 | tf_op jit(solution)/shard_map/ppermute | solution.py:28
  5.6 1.6 %collective-permute-start.3 = (bf16[1,128,1024]{2,1,0:T(8,128)(2,1)}, bf16[1,128,1024]{2,1,0:T(8,128)(2,1)S(1)}, u32[]{:S(2)}, u32[]{:S(2)}) collective-permute-start(bf16[1,128,1024]{2,1,0:T(8,128)(2,1)} %param.8), channel_id=1, source_target_pairs={{0,2},{1,3},{2,4},{3,5},{4,6},{5,7},{6,0},{7,1},{8,10},{9,11},{10,... | collective-permute-start | bytes 786440 | tf_op jit(solution)/shard_map/ppermute | solution.py:33
  7.4 0.7 %tables.1.angle_ref = f32[2,384,128]{2,1,0:T(8,128)S(1)} custom-call(f32[2,128]{1,0:T(2,128)S(1)} %pad_maximum_fusion.freq_ref), custom_call_target="tpu_custom_call" | custom-call | flops 10000000000 | bytes 100000 | tf_op jit(solution)/shard_map/tables/pallas_call | solution.py:91
  8.2 0.2 copy-done.2
  8.5 2.6 %prepare.1 = (bf16[8,256,256]{2,1,0:T(8,128)(2,1)S(1)}, f32[8,256,128]{2,1,0:T(8,128)S(1)}, f32[8,256,128]{2,1,0:T(8,128)S(1)}, bf16[8,128,256]{2,1,0:T(8,128)(2...) custom-call(bf16[128,2048]{1,0:T(8,128)(2,1)S(1)} %bitcast.27, ...), custom_call_target="tpu_custom_call" | custom-call | flops 1000000 | bytes 100000 | tf_op jit(solution)/shard_map/prepare/pallas_call | solution.py:91
  11.0 1.6 %collective-permute-done = bf16[1,128,1024]{2,1,0:T(8,128)(2,1)S(1)} collective-permute-done((bf16[1,128,1024]{2,1,0:T(8,128)(2,1)}, bf16[1,128,1024]{2,1,0:T(8,128)(2,1)S(1)}, u32[]{:S(2)}, u32[]{:S(2)}) %collective-permute-start) | collective-permute-done | bytes 262176 | tf_op jit(solution)/shard_map/ppermute | solution.py:28
  12.6 0.5 %collective-permute-start.1 = (bf16[1,128,1024]{2,1,0:T(8,128)(2,1)S(1)}, bf16[1,128,1024]{2,1,0:T(8,128)(2,1)S(1)}, u32[]{:S(2)}, u32[]{:S(2)}) collective-permute-start(bf16[1,128,1024]{2,1,0:T(8,128)(2,1)S(1)} %copy-done.3), channel_id=1, source_target_pairs={{0,1},{1,0},{2,3},{3,2},{4,5},{5,4},{6,7},{7,6},{8,9},{9,8},{10,11... | collective-permute-start | bytes 786440 | tf_op jit(solution)/shard_map/ppermute | solution.py:37
  13.1 4.0 %collective-permute-done.3 = bf16[1,128,1024]{2,1,0:T(8,128)(2,1)S(1)} collective-permute-done((bf16[1,128,1024]{2,1,0:T(8,128)(2,1)}, bf16[1,128,1024]{2,1,0:T(8,128)(2,1)S(1)}, u32[]{:S(2)}, u32[]{:S(2)}) %collective-permute-start.3) | collective-permute-done | bytes 262176 | tf_op jit(solution)/shard_map/ppermute | solution.py:33
  17.1 4.8 %scores.1 = (f32[8,384,256]{2,1,0:T(8,128)S(1)}, bf16[8,256,256]{2,1,0:T(8,128)(2,1)S(1)}, f32[8,256,128]{2,1,0:T(8,128)S(1)}, f32[128,1024]{1,0:T(8,128)S(1)}, ...) custom-call(bf16[8,256,256]{2,1,0:T(8,128)(2,1)S(1)} %get-tuple-element.38.q_ref, ...), custom_call_target="tpu_custom_call" | custom-call | flops 1000000 | bytes 100000 | tf_op jit(solution)/shard_map/scores/pallas_call | solution.py:91
  21.9 3.1 %grads.1 = (f32[8,256,128]{2,1,0:T(8,128)S(1)}, f32[128,1024]{1,0:T(8,128)S(1)}, bf16[128,1024]{1,0:T(8,128)(2,1)S(1)}, bf16[128,1024]{1,0:T(8,128)(2,1)S(1)}, f32[2,128]{1,0:T(2,128)S(1)}) custom-call(f32[8,384,256]{2,1,0:T(8,128)S(1)} %get-tuple-element.43.probs_ref, bf16[8,256,256]{2,1,0:T(8,128)(2,1)S(1)} %get-tuple-element.38.q_ref, ...), custom_call_target="tpu_custom_call" | custom-call | flops 1000000 | bytes 100000 | tf_op jit(solution)/shard_map/grads/pallas_call | solution.py:91
  25.0 0.6 %collective-permute-start.7 = (bf16[128,1024]{1,0:T(8,128)(2,1)S(1)}, bf16[128,1024]{1,0:T(8,128)(2,1)S(1)}, u32[]{:S(2)}, u32[]{:S(2)}) collective-permute-start(bf16[128,1024]{1,0:T(8,128)(2,1)S(1)} %get-tuple-element.50), channel_id=1, source_target_pairs={{0,1},{1,0},{2,3},{3,2},{4,5},{5,4},{6,7},{7,6},{8,9},{9,8},{10,11... | collective-permute-start | bytes 786440 | tf_op jit(solution)/shard_map/ppermute | solution.py:37
  25.7 2.4 %collective-permute-start.6 = (f32[2,128]{1,0:T(2,128)S(1)}, f32[2,128]{1,0:T(2,128)S(1)}, u32[]{:S(2)}, u32[]{:S(2)}) collective-permute-start(f32[2,128]{1,0:T(2,128)S(1)} %get-tuple-element.49), channel_id=1, source_target_pairs={{0,2},{1,3},{2,0},{3,1},{4,6},{5,7},{6,4},{7,5},{8,10},{9,11},{10,... | collective-permute-start | bytes 3080 | tf_op jit(solution)/shard_map/ppermute | solution.py:285
  28.0 1.6 %collective-permute-done.6 = f32[2,128]{1,0:T(2,128)S(1)} collective-permute-done((f32[2,128]{1,0:T(2,128)S(1)}, f32[2,128]{1,0:T(2,128)S(1)}, u32[]{:S(2)}, u32[]{:S(2)}) %collective-permute-start.6) | collective-permute-done | bytes 1056 | tf_op jit(solution)/shard_map/ppermute | solution.py:285
  29.8 1.3 %collective-permute-start.12 = (bf16[2,128,1024]{2,1,0:T(8,128)(2,1)S(1)}, bf16[2,128,1024]{2,1,0:T(8,128)(2,1)S(1)}, u32[]{:S(2)}, u32[]{:S(2)}) collective-permute-start(bf16[2,128,1024]{2,1,0:T(8,128)(2,1)S(1)} %merge.1), channel_id=1, source_target_pairs={{2,0},{3,1},{4,2},{5,3},{6,4},{7,5},{10,8},{11,9},{12,10},{13,11},... | collective-permute-start | bytes 1572872 | tf_op jit(solution)/shard_map/ppermute | solution.py:28
  31.1 1.6 %collective-permute-start.8 = (f32[2,128]{1,0:T(2,128)S(1)}, f32[2,128]{1,0:T(2,128)S(1)}, u32[]{:S(2)}, u32[]{:S(2)}) collective-permute-start(f32[2,128]{1,0:T(2,128)S(1)} %add.12), channel_id=1, source_target_pairs={{0,8},{8,0},{16,24},{24,16},{1,9},{9,1},{17,25},{25,17},{2,10},{10... | collective-permute-start | bytes 3080 | tf_op jit(solution)/shard_map/ppermute | solution.py:285
  32.6 2.1 %collective-permute-done.8 = f32[2,128]{1,0:T(2,128)S(1)} collective-permute-done((f32[2,128]{1,0:T(2,128)S(1)}, f32[2,128]{1,0:T(2,128)S(1)}, u32[]{:S(2)}, u32[]{:S(2)}) %collective-permute-start.8) | collective-permute-done | bytes 1056 | tf_op jit(solution)/shard_map/ppermute | solution.py:285
  34.7 1.5 %collective-permute-start.9 = (f32[2,128]{1,0:T(2,128)S(1)}, f32[2,128]{1,0:T(2,128)S(1)}, u32[]{:S(2)}, u32[]{:S(2)}) collective-permute-start(f32[2,128]{1,0:T(2,128)S(1)} %add.13), channel_id=1, source_target_pairs={{0,16},{8,24},{16,0},{24,8},{1,17},{9,25},{17,1},{25,9},{2,18},{10... | collective-permute-start | bytes 3080 | tf_op jit(solution)/shard_map/ppermute | solution.py:285
  36.2 2.1 %collective-permute-done.9 = f32[2,128]{1,0:T(2,128)S(1)} collective-permute-done((f32[2,128]{1,0:T(2,128)S(1)}, f32[2,128]{1,0:T(2,128)S(1)}, u32[]{:S(2)}, u32[]{:S(2)}) %collective-permute-start.9) | collective-permute-done | bytes 1056 | tf_op jit(solution)/shard_map/ppermute | solution.py:285
  38.3 2.0 %outputs.1 = (bf16[128,2048]{1,0:T(8,128)(2,1)}, bf16[128,2048]{1,0:T(8,128)(2,1)}) custom-call(f32[8,384,256]{2,1,0:T(8,128)S(1)} %get-tuple-element.43.probs_ref, bf16[128,1024]{1,0:T(8,128)(2,1)S(1)} %bitcast.20, bf16[128,1024]{1,0:T(8,128)(2,1)S(1)} %bitcast.24, bf16[128,1024]{1,0:T(8,128)(2,1)S(1)} %bitcast.26, bf16[128,1024]{1,0:T(8,128)(2,1)S(1)} %bitcast.22, ...), custom_call_target="tpu_custom_call" | custom-call | flops 1000000 | bytes 100000 | tf_op jit(solution)/shard_map/outputs/pallas_call | solution.py:91
  40.3 4.7 %collective-permute-done.12.far_ref = bf16[2,128,1024]{2,1,0:T(8,128)(2,1)S(1)} collective-permute-done((bf16[2,128,1024]{2,1,0:T(8,128)(2,1)S(1)}, bf16[2,128,1024]{2,1,0:T(8,128)(2,1)S(1)}, u32[]{:S(2)}, u32[]{:S(2)}) %collective-permute-start.12) | collective-permute-done | bytes 524320 | tf_op jit(solution)/shard_map/ppermute | solution.py:28
  45.1 2.7 %collective-permute-start.13 = (f32[2,128]{1,0:T(2,128)S(1)}, f32[2,128]{1,0:T(2,128)S(1)}, u32[]{:S(2)}, u32[]{:S(2)}) collective-permute-start(f32[2,128]{1,0:T(2,128)S(1)} %add.15.own_ref), channel_id=1, source_target_pairs={{0,4},{1,5},{2,6},{3,7},{4,0},{5,1},{6,2},{7,3},{8,12},{9,13},{10,... | collective-permute-start | bytes 3080 | tf_op jit(solution)/shard_map/ppermute | solution.py:285
  47.8 1.4 %finish.1 = (bf16[128,1024]{1,0:T(8,128)(2,1)}, bf16[128,1024]{1,0:T(8,128)(2,1)}) custom-call(f32[128,1024]{1,0:T(8,128)S(1)} %get-tuple-element.62.dy_ref, f32[128,1024]{1,0:T(8,128)S(1)} %get-tuple-element.63.dv_ref, bf16[128,1024]{1,0:T(8,128)(2,1)S(1)} %collective-permute-done.7.k_near_ref.k1_ref, ...), custom_call_target="tpu_custom_call" | custom-call | flops 1000000 | bytes 100000 | tf_op jit(solution)/shard_map/finish/pallas_call | solution.py:91
  49.2 0.3 collective-permute-done.13.other_ref
  49.5 0.8 %share.1 = f32[1,64]{1,0:T(1,128)} custom-call(f32[2,128]{1,0:T(2,128)S(1)} %add.15.own_ref, f32[2,128]{1,0:T(2,128)S(1)} %collective-permute-done.13.other_ref), custom_call_target="tpu_custom_call" | custom-call | flops 1000000 | bytes 100000 | tf_op jit(solution)/shard_map/share/pallas_call | solution.py:91
  (33 shorter events, 0.5 us)
Async XLA Ops:
  0.6 12.0 %collective-permute-start = (bf16[1,128,1024]{2,1,0:T(8,128)(2,1)}, bf16[1,128,1024]{2,1,0:T(8,128)(2,1)S(1)}, u32[]{:S(2)}, u32[]{:S(2)}) collective-permute-start(bf16[1,128,1024]{2,1,0:T(8,128)(2,1)} %param.7), channel_id=1, source_target_pairs={{0,2},{1,3},{2,4},{3,5},{4,6},{5,7},{8,10},{9,11},{10,12},{11,13},... | collective-permute-start | bytes 786440 | tf_op jit(solution)/shard_map/ppermute | solution.py:28
  5.6 11.5 %collective-permute-start.3 = (bf16[1,128,1024]{2,1,0:T(8,128)(2,1)}, bf16[1,128,1024]{2,1,0:T(8,128)(2,1)S(1)}, u32[]{:S(2)}, u32[]{:S(2)}) collective-permute-start(bf16[1,128,1024]{2,1,0:T(8,128)(2,1)} %param.8), channel_id=1, source_target_pairs={{0,2},{1,3},{2,4},{3,5},{4,6},{5,7},{6,0},{7,1},{8,10},{9,11},{10,... | collective-permute-start | bytes 786440 | tf_op jit(solution)/shard_map/ppermute | solution.py:33
  7.3 1.0 %copy-start.2 = (bf16[1,128,2048]{2,1,0:T(8,128)(2,1)S(1)}, bf16[1,128,2048]{2,1,0:T(8,128)(2,1)}, u32[]{:S(2)}) copy-start(bf16[1,128,2048]{2,1,0:T(8,128)(2,1)} %param.6) | copy-start | bytes 1572868
  7.3 1.1 %copy-start.3 = (bf16[1,128,1024]{2,1,0:T(8,128)(2,1)S(1)}, bf16[1,128,1024]{2,1,0:T(8,128)(2,1)}, u32[]{:S(2)}) copy-start(bf16[1,128,1024]{2,1,0:T(8,128)(2,1)} %param.7) | copy-start | bytes 786436
  7.4 1.1 %copy-start.4 = (f32[128]{0:T(128)S(1)}, f32[128]{0:T(128)}, u32[]{:S(2)}) copy-start(f32[128]{0:T(128)} %param.11) | copy-start | bytes 1540
  7.4 1.1 %copy-start.5 = (f32[128]{0:T(128)S(1)}, f32[128]{0:T(128)}, u32[]{:S(2)}) copy-start(f32[128]{0:T(128)} %param.10) | copy-start | bytes 1540
  7.4 5.7 %copy-start.1 = (bf16[1,128,1024]{2,1,0:T(8,128)(2,1)S(1)}, bf16[1,128,1024]{2,1,0:T(8,128)(2,1)}, u32[]{:S(2)}) copy-start(bf16[1,128,1024]{2,1,0:T(8,128)(2,1)} %param.8) | copy-start | bytes 786436
  7.4 9.7 %copy-start = (bf16[1,128,2048]{2,1,0:T(8,128)(2,1)S(1)}, bf16[1,128,2048]{2,1,0:T(8,128)(2,1)}, u32[]{:S(2)}) copy-start(bf16[1,128,2048]{2,1,0:T(8,128)(2,1)} %param.9) | copy-start | bytes 1572868
  12.6 4.5 %collective-permute-start.2 = (bf16[1,128,1024]{2,1,0:T(8,128)(2,1)S(1)}, bf16[1,128,1024]{2,1,0:T(8,128)(2,1)S(1)}, u32[]{:S(2)}, u32[]{:S(2)}) collective-permute-start(bf16[1,128,1024]{2,1,0:T(8,128)(2,1)S(1)} %collective-permute-done), channel_id=1, source_target_pairs={{0,1},{1,0},{2,3},{3,2},{4,5},{5,4},{6,7},{7,6},{8,9},{9,8},{10,11... | collective-permute-start | bytes 786440 | tf_op jit(solution)/shard_map/ppermute | solution.py:37
  12.6 4.5 %collective-permute-start.1 = (bf16[1,128,1024]{2,1,0:T(8,128)(2,1)S(1)}, bf16[1,128,1024]{2,1,0:T(8,128)(2,1)S(1)}, u32[]{:S(2)}, u32[]{:S(2)}) collective-permute-start(bf16[1,128,1024]{2,1,0:T(8,128)(2,1)S(1)} %copy-done.3), channel_id=1, source_target_pairs={{0,1},{1,0},{2,3},{3,2},{4,5},{5,4},{6,7},{7,6},{8,9},{9,8},{10,11... | collective-permute-start | bytes 786440 | tf_op jit(solution)/shard_map/ppermute | solution.py:37
  13.1 8.8 %collective-permute-start.4 = (bf16[1,128,1024]{2,1,0:T(8,128)(2,1)S(1)}, bf16[1,128,1024]{2,1,0:T(8,128)(2,1)S(1)}, u32[]{:S(2)}, u32[]{:S(2)}) collective-permute-start(bf16[1,128,1024]{2,1,0:T(8,128)(2,1)S(1)} %copy-done.1), channel_id=1, source_target_pairs={{0,1},{1,0},{2,3},{3,2},{4,5},{5,4},{6,7},{7,6},{8,9},{9,8},{10,11... | collective-permute-start | bytes 786440 | tf_op jit(solution)/shard_map/ppermute | solution.py:37
  17.1 4.8 %collective-permute-start.5 = (bf16[1,128,1024]{2,1,0:T(8,128)(2,1)S(1)}, bf16[1,128,1024]{2,1,0:T(8,128)(2,1)S(1)}, u32[]{:S(2)}, u32[]{:S(2)}) collective-permute-start(bf16[1,128,1024]{2,1,0:T(8,128)(2,1)S(1)} %collective-permute-done.3), channel_id=1, source_target_pairs={{0,1},{1,0},{2,3},{3,2},{4,5},{5,4},{6,7},{7,6},{8,9},{9,8},{10,11... | collective-permute-start | bytes 786440 | tf_op jit(solution)/shard_map/ppermute | solution.py:37
  25.0 4.6 %collective-permute-start.7 = (bf16[128,1024]{1,0:T(8,128)(2,1)S(1)}, bf16[128,1024]{1,0:T(8,128)(2,1)S(1)}, u32[]{:S(2)}, u32[]{:S(2)}) collective-permute-start(bf16[128,1024]{1,0:T(8,128)(2,1)S(1)} %get-tuple-element.50), channel_id=1, source_target_pairs={{0,1},{1,0},{2,3},{3,2},{4,5},{5,4},{6,7},{7,6},{8,9},{9,8},{10,11... | collective-permute-start | bytes 786440 | tf_op jit(solution)/shard_map/ppermute | solution.py:37
  25.6 4.0 %collective-permute-start.11 = (bf16[128,1024]{1,0:T(8,128)(2,1)S(1)}, bf16[128,1024]{1,0:T(8,128)(2,1)S(1)}, u32[]{:S(2)}, u32[]{:S(2)}) collective-permute-start(bf16[128,1024]{1,0:T(8,128)(2,1)S(1)} %get-tuple-element.55), channel_id=1, source_target_pairs={{0,1},{1,0},{2,3},{3,2},{4,5},{5,4},{6,7},{7,6},{8,9},{9,8},{10,11... | collective-permute-start | bytes 786440 | tf_op jit(solution)/shard_map/ppermute | solution.py:37
  25.7 3.9 %collective-permute-start.6 = (f32[2,128]{1,0:T(2,128)S(1)}, f32[2,128]{1,0:T(2,128)S(1)}, u32[]{:S(2)}, u32[]{:S(2)}) collective-permute-start(f32[2,128]{1,0:T(2,128)S(1)} %get-tuple-element.49), channel_id=1, source_target_pairs={{0,2},{1,3},{2,0},{3,1},{4,6},{5,7},{6,4},{7,5},{8,10},{9,11},{10,... | collective-permute-start | bytes 3080 | tf_op jit(solution)/shard_map/ppermute | solution.py:285
  29.8 15.3 %collective-permute-start.12 = (bf16[2,128,1024]{2,1,0:T(8,128)(2,1)S(1)}, bf16[2,128,1024]{2,1,0:T(8,128)(2,1)S(1)}, u32[]{:S(2)}, u32[]{:S(2)}) collective-permute-start(bf16[2,128,1024]{2,1,0:T(8,128)(2,1)S(1)} %merge.1), channel_id=1, source_target_pairs={{2,0},{3,1},{4,2},{5,3},{6,4},{7,5},{10,8},{11,9},{12,10},{13,11},... | collective-permute-start | bytes 1572872 | tf_op jit(solution)/shard_map/ppermute | solution.py:28
  31.1 3.6 %collective-permute-start.8 = (f32[2,128]{1,0:T(2,128)S(1)}, f32[2,128]{1,0:T(2,128)S(1)}, u32[]{:S(2)}, u32[]{:S(2)}) collective-permute-start(f32[2,128]{1,0:T(2,128)S(1)} %add.12), channel_id=1, source_target_pairs={{0,8},{8,0},{16,24},{24,16},{1,9},{9,1},{17,25},{25,17},{2,10},{10... | collective-permute-start | bytes 3080 | tf_op jit(solution)/shard_map/ppermute | solution.py:285
  34.7 3.6 %collective-permute-start.9 = (f32[2,128]{1,0:T(2,128)S(1)}, f32[2,128]{1,0:T(2,128)S(1)}, u32[]{:S(2)}, u32[]{:S(2)}) collective-permute-start(f32[2,128]{1,0:T(2,128)S(1)} %add.13), channel_id=1, source_target_pairs={{0,16},{8,24},{16,0},{24,8},{1,17},{9,25},{17,1},{25,9},{2,18},{10... | collective-permute-start | bytes 3080 | tf_op jit(solution)/shard_map/ppermute | solution.py:285
  38.3 2.0 %collective-permute-start.10 = (f32[2,128]{1,0:T(2,128)S(1)}, f32[2,128]{1,0:T(2,128)S(1)}, u32[]{:S(2)}, u32[]{:S(2)}) collective-permute-start(f32[2,128]{1,0:T(2,128)S(1)} %add.14), channel_id=1, source_target_pairs={{0,1},{1,0},{2,3},{3,2},{4,5},{5,4},{6,7},{7,6},{8,9},{9,8},{10,11... | collective-permute-start | bytes 3080 | tf_op jit(solution)/shard_map/ppermute | solution.py:285
  45.1 4.5 %collective-permute-start.13 = (f32[2,128]{1,0:T(2,128)S(1)}, f32[2,128]{1,0:T(2,128)S(1)}, u32[]{:S(2)}, u32[]{:S(2)}) collective-permute-start(f32[2,128]{1,0:T(2,128)S(1)} %add.15.own_ref), channel_id=1, source_target_pairs={{0,4},{1,5},{2,6},{3,7},{4,0},{5,1},{6,2},{7,3},{8,12},{9,13},{10,... | collective-permute-start | bytes 3080 | tf_op jit(solution)/shard_map/ppermute | solution.py:285

commit v3 on v2

--- a/solution.py
+++ b/solution.py
@@ -16,7 +16,6 @@
 GROUP = 2
 F32 = jnp.float32
 BF16 = jnp.bfloat16
-UNROLL = 8
 TABLES_COST = 10_000_000_000
 IN_VMEM = pl.BlockSpec(memory_space=pltpu.VMEM)
 VMEM_LIMIT = 24 * 1024 * 1024
@@ -71,7 +70,7 @@
 
 
 def columns(index, size):
-    return pl.ds(pl.multiple_of(index * size, size), size)
+    return slice(index * size, (index + 1) * size)
 
 
 def stacked(ref, h, head):
@@ -79,12 +78,8 @@
 
 
 def each_head(count, body):
-    def several(i, carry):
-        for u in range(UNROLL):
-            body(i * UNROLL + u)
-        return carry
-
-    lax.fori_loop(0, count // UNROLL, several, 0)
+    for h in range(count):
+        body(h)
 
 
 def call(kernel, name, outs, args, flops=1_000_000, traffic=100_000, scratch=()):
@@ -145,7 +140,7 @@
 
 
 def scores_kernel(
-    q_ref, do_ref, own_ref, k1a_ref, k1b_ref, k2_ref, turn_ref,
+    q_ref, do_ref, own_ref, k1a_ref, k1b_ref, k1c_ref, k2_ref, turn_ref,
     probs_ref, keys_ref, unit_ref, dv_ref, dv1_ref, dv2_ref,
 ):
     heads, span, _ = probs_ref.shape
@@ -162,7 +157,9 @@
 
     def body(h):
         cols = columns(h, head)
-        raw = jnp.concatenate([k2_ref[:, cols], jnp.where(odd, k1a_ref[:, cols], k1b_ref[:, cols])], axis=0)
+        half_ref, low = (k1b_ref, h) if h < heads // 2 else (k1c_ref, h - heads // 2)
+        near = jnp.where(odd, k1a_ref[:, cols], half_ref[:, columns(low, head)])
+        raw = jnp.concatenate([k2_ref[:, cols], near], axis=0)
         rotated, swapped, normed, _ = norm_rotate(raw, turn, turn_s, swap)
         keys_ref[h, :, :head] = rotated
         keys_ref[h, :, head:] = swapped
@@ -184,7 +181,7 @@
 def grads_kernel(
     probs_ref, q_ref, q_unit_ref, do_ref, keys_ref, own_ref, unit_ref, own_unit_ref, v0_ref, v1a_ref, v1b_ref, v2_ref,
     angle_ref,
-    dqy_ref, dy_ref, dk1_ref, dk2_ref, sum_ref, dg_ref,
+    dqy_ref, dy_ref, dk1a_ref, dk1b_ref, dk2_ref, sum_ref, dg_ref,
 ):
     heads, span, _ = probs_ref.shape
     rows, head = own_ref.shape[1], own_ref.shape[2] // 2
@@ -207,7 +204,8 @@
         d_query = dot(d_score, jnp.concatenate([keys_ref[h], own_ref[h]], axis=0), ((0,), (0,)))
 
         dk2_ref[:, cols] = d_key[: far - rows, :head].astype(BF16)
-        dk1_ref[:, cols] = d_key[far - rows : far, :head].astype(BF16)
+        dk1_ref, low = (dk1a_ref, h) if h < heads // 2 else (dk1b_ref, h - heads // 2)
+        dk1_ref[:, columns(low, head)] = d_key[far - rows : far, :head].astype(BF16)
         term = d_key[:far].astype(BF16).astype(F32)
         d_y_far = term[:, :head] * cosine[:far] - term[:, head:] * sine[:far]
         d_y_own = d_key[far:, :head] * cosine[far:] - d_key[far:, head:] * sine[far:]
@@ -242,14 +240,18 @@
     each_head(heads, body)
 
 
-def merge_kernel(k_far_ref, k_near_ref, v_far_ref, v_near_ref, out_ref):
-    odd = lax.rem(lax.axis_index("ctx"), 2) == 1
-    for i, (far_ref, near_ref) in enumerate(((k_far_ref, k_near_ref), (v_far_ref, v_near_ref))):
+def merge_kernel(far_ref, *refs):
+    near_refs, out_ref = refs[:-1], refs[-1]
+    odd = lax.rem(lax.axis_index("ctx"), 2) == 1
+    low = 0
+    for near_ref in near_refs:
+        cols = slice(low, low + near_ref.shape[1])
         near = jnp.where(odd, near_ref[...].astype(F32), 0.0)
-        out_ref[i] = (far_ref[...].astype(F32) + near).astype(BF16)
-
-
-def finish_kernel(dy_ref, dv_ref, k1_ref, v1_ref, far_ref, unit_ref, inv_ref, angle_ref, gain_ref, dk_out, dv_out):
+        out_ref[:, cols] = (far_ref[:, cols].astype(F32) + near).astype(BF16)
+        low = cols.stop
+
+
+def finish_kernel(dy_ref, dv_ref, k1a_ref, k1b_ref, v1_ref, k2_ref, v2_ref, unit_ref, inv_ref, angle_ref, gain_ref, dk_out, dv_out):
     heads, rows, head = unit_ref.shape
     far = angle_ref.shape[1] - rows
     odd = lax.rem(lax.axis_index("ctx"), 2) == 1
@@ -261,9 +263,10 @@
     def body(h):
         cols = columns(h, head)
         near = jnp.where(odd, 0.0, v1_ref[:, cols].astype(F32))
-        dv_out[:, cols] = (dv_ref[:, cols] + near + far_ref[1, :, cols].astype(F32)).astype(BF16)
-        near = jnp.where(odd, 0.0, k1_ref[:, cols].astype(F32))
-        rest = far_ref[0, :, cols]
+        dv_out[:, cols] = (dv_ref[:, cols] + near + v2_ref[:, cols].astype(F32)).astype(BF16)
+        k1_ref, low = (k1a_ref, h) if h < heads // 2 else (k1b_ref, h - heads // 2)
+        near = jnp.where(odd, 0.0, k1_ref[:, columns(low, head)].astype(F32))
+        rest = k2_ref[:, cols]
         swapped = dot(jnp.concatenate([near.astype(BF16), rest], axis=1), swaps)
         d_y = dy_ref[:, cols] + ((near + rest.astype(F32)) * cosine - swapped * sine)
         dk_out[:, cols] = norm_back(d_y, unit_ref[h], inv_ref[h], gain).astype(BF16)
@@ -328,9 +331,7 @@
         (q_proj[0], k_proj[0], q_gain, k_gain, angle_table),
     )
     q_rot, k2 = lax.optimization_barrier((q_rot, k2))
-    k1_even, v2 = lax.optimization_barrier((swap_pairs(k2), v2))
-    k1 = k1_odd[0], k1_even[0]
-    v1 = v1_odd[0], swap_pairs(v2)[0]
+    k1 = k1_odd[0], swap_pairs(k2[0, :, : width // 2]), swap_pairs(k2[0, :, width // 2 :])
     probs, far_keys, far_unit, dv_own, dv1, dv2 = call(
         scores_kernel,
         "scores",
@@ -338,37 +339,41 @@
         + [((rows, width), F32), ((rows, width), BF16), ((rows, width), BF16)],
         (q_rot, d_out[0], k_rot, *k1, k2[0], turn_table),
     )
+    v2, dv1, dv2 = lax.optimization_barrier((v2, dv1, dv2))
+    v1 = v1_odd[0], swap_pairs(v2)[0]
     dv_near = swap_pairs(dv1)
-    dq_y, dy_own, dk1, dk2, gain_terms = call(
+    (v_merged,) = call(merge_kernel, "merge_v", [((rows, width), BF16)], (dv2, dv_near))
+    v_back = hop(v_merged, -2)
+    dq_y, dy_own, dk1a, dk1b, dk2, gain_terms = call(
         grads_kernel,
         "grads",
-        [((heads, tall, head), F32), ((rows, width), F32), ((rows, width), BF16), ((rows, width), BF16)]
-        + [((2, head), F32)],
+        [((heads, tall, head), F32), ((rows, width), F32), ((rows, width // 2), BF16), ((rows, width // 2), BF16)]
+        + [((rows, width), BF16), ((2, head), F32)],
         (probs, q_rot, q_unit, d_out[0], far_keys, k_rot, far_unit, k_unit, v_proj[0], *v1, v2[0], angle_table),
         scratch=[pltpu.VMEM((16, head), F32)],
     )
-    dk_near = swap_pairs(dk1)
+    dk_near = swap_pairs(dk1a), swap_pairs(dk1b)
+    gain_terms = all_sum(gain_terms, "ctx", [1])
     gain_terms = all_sum(gain_terms, "ctx", [2])
-    gain_terms, dk_near = lax.optimization_barrier((gain_terms, dk_near))
-    (merged,) = call(merge_kernel, "merge", [((2, rows, width), BF16)], (dk2, dk_near, dv2, dv_near))
-    back = hop(merged, -2)
-    gain_terms = all_sum(all_sum(gain_terms, "dp", doublings("dp")), "ctx", [1])
+    gain_terms, dk_near, v_back = lax.optimization_barrier((gain_terms, dk_near, v_back))
+    (merged,) = call(merge_kernel, "merge_k", [((rows, width), BF16)], (dk2, *dk_near))
+    k_back = hop(merged, -2)
+    gain_terms = all_sum(gain_terms, "dp", doublings("dp"))
     result, d_q = call(
         outputs_kernel,
         "outputs",
         [((rows, wide), BF16), ((rows, wide), BF16)],
         (probs, v_proj[0], *v1, v2[0], dq_y, q_unit, q_inv, q_gain),
     )
-    gain_terms, back, result, d_q = lax.optimization_barrier((gain_terms, back, result, d_q))
-    for step in doublings("ctx", 4)[:-1]:
-        gain_terms = all_sum(gain_terms, "ctx", [step])
-    last = doublings("ctx", 4)[-1]
+    gain_terms, k_back, result, d_q = lax.optimization_barrier((gain_terms, k_back, result, d_q))
+    *steps, last = doublings("ctx", 4)
+    gain_terms = all_sum(gain_terms, "ctx", steps)
     others = all_sum_term(gain_terms, "ctx", last)
     d_k, d_v = call(
         finish_kernel,
         "finish",
         [((rows, width), BF16), ((rows, width), BF16)],
-        (dy_own, dv_own, dk_near, dv_near, back, k_unit, k_inv, angle_table, k_gain),
+        (dy_own, dv_own, *dk_near, dv_near, k_back, v_back, k_unit, k_inv, angle_table, k_gain),
     )
     share = 2 * head // lax.axis_size("dp")
     (gain_share,) = call(share_kernel, "share", [((1, share), F32)], (gain_terms, others))

time: 50.5 us -> 47.3 us (0.937)
  waiting for transfers between devices: 16.3 us -> 9.83 us
  starting transfers between devices: 17.2 us -> 20.4 us
    ppermute x1, waiting for transfers between devices: 3.97 us -> 0.01 us  [ring_hop(): lax.ppermute(value, 'ctx', [(i, (i + steps) % count) for i in range(count)])]
    ppermute x2 -> x3, waiting for transfers between devices: 6.3 us -> 2.85 us  [hop(): lax.ppermute(value, 'ctx', [(i, i + steps) for i in range(initial, last)])]
    ppermute x6 -> x8, waiting for transfers between devices: 0.02 us -> 1.73 us  [swap_pairs(): lax.ppermute(value, 'ctx', [(i, i ^ 1) for i in range(lax.axis_size('ctx'...]
    ppermute x6 -> x8, starting transfers between devices: 1.16 us -> 2.6 us  [swap_pairs(): lax.ppermute(value, 'ctx', [(i, i ^ 1) for i in range(lax.axis_size('ctx'...]
    ppermute x5, starting transfers between devices: 8.2 us -> 9.12 us  [all_sum_term(): lax.ppermute(value, axis, [(i, i ^ step) for i in range(lax.axis_size(axi...]
    ppermute x2 -> x3, starting transfers between devices: 6.27 us -> 7.08 us  [hop(): lax.ppermute(value, 'ctx', [(i, i + steps) for i in range(initial, last)])]
    ppermute x5, waiting for transfers between devices: 6 us -> 5.24 us  [all_sum_term(): lax.ppermute(value, axis, [(i, i ^ step) for i in range(lax.axis_size(axi...]
    pallas_call x8 -> x9, Pallas kernels: 15.6 us -> 15.6 us  [call(): pl.pallas_call(kernel, name=name, in_specs=[IN_VMEM] * len(args), out_spe...]
  transfers between devices with their start and end apart: 14 -> 17, of which waited for: 7 -> 9; matrix products, arithmetic and copies ran while one was open for 0% -> 0% of each run, Pallas kernels for 23% -> 31%
where the time goes in v3:
time: 47.3 us; the launch traced here: 47.1 us
  starting transfers between devices  20.4 us (43%)
  Pallas kernels  15.6 us (33%)
  waiting for transfers between devices  9.83 us (21%)
  between operations  0.8 us (2%)
    pallas_call x9, Pallas kernels, call(): pl.pallas_call(kernel, name=name, in_specs=[IN_VMEM] * len(args), out_spe...  15.6 us
    ppermute x5, starting transfers between devices, all_sum_term(): lax.ppermute(value, axis, [(i, i ^ step) for i in range(lax.axis_size(axi...  9.12 us
    ppermute x3, starting transfers between devices, hop(): lax.ppermute(value, 'ctx', [(i, i + steps) for i in range(initial, last)])  7.08 us
    ppermute x5, waiting for transfers between devices, all_sum_term(): lax.ppermute(value, axis, [(i, i ^ step) for i in range(lax.axis_size(axi...  5.24 us
    ppermute x3, waiting for transfers between devices, hop(): lax.ppermute(value, 'ctx', [(i, i + steps) for i in range(initial, last)])  2.85 us
    ppermute x8, starting transfers between devices, swap_pairs(): lax.ppermute(value, 'ctx', [(i, i ^ 1) for i in range(lax.axis_size('ctx'...  2.6 us
    ppermute x8, waiting for transfers between devices, swap_pairs(): lax.ppermute(value, 'ctx', [(i, i ^ 1) for i in range(lax.axis_size('ctx'...  1.73 us
    ppermute x1, starting transfers between devices, ring_hop(): lax.ppermute(value, 'ctx', [(i, (i + steps) % count) for i in range(count)])  1.62 us
  transfers between devices with their start and end apart: 17, of which 9 were waited for; matrix products, arithmetic and copies ran while one was open for 0% of the time, Pallas kernels for 31%

profile of v3, /device:TPU:0, one launch (start us, length us, event | category | flops | bytes accessed | tf_op | source)
XLA Modules:
  0.0 47.1 jit_solution(1423414639898745710)
XLA Ops:
  0.6 0.6 %collective-permute-start.1 = (bf16[1,128,1024]{2,1,0:T(8,128)(2,1)}, bf16[1,128,1024]{2,1,0:T(8,128)(2,1)S(1)}, u32[]{:S(2)}, u32[]{:S(2)}) collective-permute-start(bf16[1,128,1024]{2,1,0:T(8,128)(2,1)} %param.7), channel_id=1, source_target_pairs={{0,1},{1,0},{2,3},{3,2},{4,5},{5,4},{6,7},{7,6},{8,9},{9,8},{10,11... | collective-permute-start | bytes 786440 | tf_op jit(solution)/shard_map/ppermute | solution.py:36
  1.2 4.5 %collective-permute-start = (bf16[1,128,1024]{2,1,0:T(8,128)(2,1)}, bf16[1,128,1024]{2,1,0:T(8,128)(2,1)S(1)}, u32[]{:S(2)}, u32[]{:S(2)}) collective-permute-start(bf16[1,128,1024]{2,1,0:T(8,128)(2,1)} %param.7), channel_id=1, source_target_pairs={{0,2},{1,3},{2,4},{3,5},{4,6},{5,7},{8,10},{9,11},{10,12},{11,13},... | collective-permute-start | bytes 786440 | tf_op jit(solution)/shard_map/ppermute | solution.py:27
  5.7 1.6 %collective-permute-start.5 = (bf16[1,128,1024]{2,1,0:T(8,128)(2,1)}, bf16[1,128,1024]{2,1,0:T(8,128)(2,1)S(1)}, u32[]{:S(2)}, u32[]{:S(2)}) collective-permute-start(bf16[1,128,1024]{2,1,0:T(8,128)(2,1)} %param.8), channel_id=1, source_target_pairs={{0,2},{1,3},{2,4},{3,5},{4,6},{5,7},{6,0},{7,1},{8,10},{9,11},{10,... | collective-permute-start | bytes 786440 | tf_op jit(solution)/shard_map/ppermute | solution.py:32
  7.5 0.7 %tables.1.angle_ref = f32[2,384,128]{2,1,0:T(8,128)S(1)} custom-call(f32[2,128]{1,0:T(2,128)S(1)} %pad_maximum_fusion.freq_ref), custom_call_target="tpu_custom_call" | custom-call | flops 10000000000 | bytes 100000 | tf_op jit(solution)/shard_map/tables/pallas_call | solution.py:86
  8.5 2.6 %prepare.1 = (bf16[8,256,256]{2,1,0:T(8,128)(2,1)S(1)}, f32[8,256,128]{2,1,0:T(8,128)S(1)}, f32[8,256,128]{2,1,0:T(8,128)S(1)}, bf16[8,128,256]{2,1,0:T(8,128)(2...) custom-call(bf16[128,2048]{1,0:T(8,128)(2,1)S(1)} %bitcast.31, ...), custom_call_target="tpu_custom_call" | custom-call | flops 1000000 | bytes 100000 | tf_op jit(solution)/shard_map/prepare/pallas_call | solution.py:86
  11.1 1.6 %collective-permute-done = bf16[1,128,1024]{2,1,0:T(8,128)(2,1)S(1)} collective-permute-done((bf16[1,128,1024]{2,1,0:T(8,128)(2,1)}, bf16[1,128,1024]{2,1,0:T(8,128)(2,1)S(1)}, u32[]{:S(2)}, u32[]{:S(2)}) %collective-permute-start) | collective-permute-done | bytes 262176 | tf_op jit(solution)/shard_map/ppermute | solution.py:27
  12.8 0.5 %collective-permute-start.2 = (bf16[128,512]{1,0:T(8,128)(2,1)S(1)}, bf16[128,512]{1,0:T(8,128)(2,1)S(1)}, u32[]{:S(2)}, u32[]{:S(2)}) collective-permute-start(bf16[128,512]{1,0:T(8,128)(2,1)S(1)} %get-tuple-element.78), channel_id=1, source_target_pairs={{0,1},{1,0},{2,3},{3,2},{4,5},{5,4},{6,7},{7,6},{8,9},{9,8},{10,11... | collective-permute-start | bytes 393224 | tf_op jit(solution)/shard_map/ppermute | solution.py:36
  13.3 0.8 %collective-permute-done.3.k1c_ref = bf16[128,512]{1,0:T(8,128)(2,1)S(1)} collective-permute-done((bf16[128,512]{1,0:T(8,128)(2,1)S(1)}, bf16[128,512]{1,0:T(8,128)(2,1)S(1)}, u32[]{:S(2)}, u32[]{:S(2)}) %collective-permute-start.3) | collective-permute-done | bytes 131104 | tf_op jit(solution)/shard_map/ppermute | solution.py:36
  14.3 4.8 %scores.1 = (f32[8,384,256]{2,1,0:T(8,128)S(1)}, bf16[8,256,256]{2,1,0:T(8,128)(2,1)S(1)}, f32[8,256,128]{2,1,0:T(8,128)S(1)}, f32[128,1024]{1,0:T(8,128)S(1)}, ...) custom-call(bf16[8,256,256]{2,1,0:T(8,128)(2,1)S(1)} %get-tuple-element.42.q_ref, ...), custom_call_target="tpu_custom_call" | custom-call | flops 1000000 | bytes 100000 | tf_op jit(solution)/shard_map/scores/pallas_call | solution.py:86
  20.0 0.7 %collective-permute-done.11.refs_0_.v1_ref = bf16[128,1024]{1,0:T(8,128)(2,1)S(1)} collective-permute-done((bf16[128,1024]{1,0:T(8,128)(2,1)S(1)}, bf16[128,1024]{1,0:T(8,128)(2,1)S(1)}, u32[]{:S(2)}, u32[]{:S(2)}) %collective-permute-start.11) | collective-permute-done | bytes 262176 | tf_op jit(solution)/shard_map/ppermute | solution.py:36
  20.8 1.3 %collective-permute-start.12 = (bf16[128,1024]{1,0:T(8,128)(2,1)S(1)}, bf16[128,1024]{1,0:T(8,128)(2,1)S(1)}, u32[]{:S(2)}, u32[]{:S(2)}) collective-permute-start(bf16[128,1024]{1,0:T(8,128)(2,1)S(1)} %merge_v.1), channel_id=1, source_target_pairs={{2,0},{3,1},{4,2},{5,3},{6,4},{7,5},{10,8},{11,9},{12,10},{13,11},... | collective-permute-start | bytes 786440 | tf_op jit(solution)/shard_map/ppermute | solution.py:27
  22.1 3.1 %grads.1 = (f32[8,256,128]{2,1,0:T(8,128)S(1)}, f32[128,1024]{1,0:T(8,128)S(1)}, bf16[128,512]{1,0:T(8,128)(2,1)S(1)}, bf16[128,512]{1,0:T(8,128)(2,1)S(1)}, bf1...) custom-call(f32[8,384,256]{2,1,0:T(8,128)S(1)} %get-tuple-element.46.probs_ref, ...), custom_call_target="tpu_custom_call" | custom-call | flops 1000000 | bytes 100000 | tf_op jit(solution)/shard_map/grads/pallas_call | solution.py:86
  26.1 0.8 %collective-permute-done.7 = f32[2,128]{1,0:T(2,128)S(1)} collective-permute-done((f32[2,128]{1,0:T(2,128)S(1)}, f32[2,128]{1,0:T(2,128)S(1)}, u32[]{:S(2)}, u32[]{:S(2)}) %collective-permute-start.7) | collective-permute-done | bytes 1056 | tf_op jit(solution)/shard_map/ppermute | solution.py:288
  27.0 3.0 %collective-permute-start.8 = (f32[2,128]{1,0:T(2,128)S(1)}, f32[2,128]{1,0:T(2,128)S(1)}, u32[]{:S(2)}, u32[]{:S(2)}) collective-permute-start(f32[2,128]{1,0:T(2,128)S(1)} %add.12), channel_id=1, source_target_pairs={{0,2},{1,3},{2,0},{3,1},{4,6},{5,7},{6,4},{7,5},{8,10},{9,11},{10,... | collective-permute-start | bytes 3080 | tf_op jit(solution)/shard_map/ppermute | solution.py:288
  30.0 1.9 %collective-permute-done.8 = f32[2,128]{1,0:T(2,128)S(1)} collective-permute-done((f32[2,128]{1,0:T(2,128)S(1)}, f32[2,128]{1,0:T(2,128)S(1)}, u32[]{:S(2)}, u32[]{:S(2)}) %collective-permute-start.8) | collective-permute-done | bytes 1056 | tf_op jit(solution)/shard_map/ppermute | solution.py:288
  32.0 1.3 %collective-permute-start.15 = (bf16[128,1024]{1,0:T(8,128)(2,1)S(1)}, bf16[128,1024]{1,0:T(8,128)(2,1)S(1)}, u32[]{:S(2)}, u32[]{:S(2)}) collective-permute-start(bf16[128,1024]{1,0:T(8,128)(2,1)S(1)} %merge_k.1), channel_id=1, source_target_pairs={{2,0},{3,1},{4,2},{5,3},{6,4},{7,5},{10,8},{11,9},{12,10},{13,11},... | collective-permute-start | bytes 786440 | tf_op jit(solution)/shard_map/ppermute | solution.py:27
  33.3 1.6 %collective-permute-start.13 = (f32[2,128]{1,0:T(2,128)S(1)}, f32[2,128]{1,0:T(2,128)S(1)}, u32[]{:S(2)}, u32[]{:S(2)}) collective-permute-start(f32[2,128]{1,0:T(2,128)S(1)} %add.13), channel_id=1, source_target_pairs={{0,8},{8,0},{16,24},{24,16},{1,9},{9,1},{17,25},{25,17},{2,10},{10... | collective-permute-start | bytes 3080 | tf_op jit(solution)/shard_map/ppermute | solution.py:288
  34.9 2.1 %collective-permute-done.13 = f32[2,128]{1,0:T(2,128)S(1)} collective-permute-done((f32[2,128]{1,0:T(2,128)S(1)}, f32[2,128]{1,0:T(2,128)S(1)}, u32[]{:S(2)}, u32[]{:S(2)}) %collective-permute-start.13) | collective-permute-done | bytes 1056 | tf_op jit(solution)/shard_map/ppermute | solution.py:288
  37.0 1.5 %collective-permute-start.14 = (f32[2,128]{1,0:T(2,128)S(1)}, f32[2,128]{1,0:T(2,128)S(1)}, u32[]{:S(2)}, u32[]{:S(2)}) collective-permute-start(f32[2,128]{1,0:T(2,128)S(1)} %add.14), channel_id=1, source_target_pairs={{0,16},{8,24},{16,0},{24,8},{1,17},{9,25},{17,1},{25,9},{2,18},{10... | collective-permute-start | bytes 3080 | tf_op jit(solution)/shard_map/ppermute | solution.py:288
  38.5 2.0 %outputs.1 = (bf16[128,2048]{1,0:T(8,128)(2,1)}, bf16[128,2048]{1,0:T(8,128)(2,1)}) custom-call(f32[8,384,256]{2,1,0:T(8,128)S(1)} %get-tuple-element.46.probs_ref, bf16[128,1024]{1,0:T(8,128)(2,1)S(1)} %bitcast.24, bf16[128,1024]{1,0:T(8,128)(2,1)S(1)} %bitcast.28, bf16[128,1024]{1,0:T(8,128)(2,1)S(1)} %bitcast.30, bf16[128,1024]{1,0:T(8,128)(2,1)S(1)} %bitcast.26, ...), custom_call_target="tpu_custom_call" | custom-call | flops 1000000 | bytes 100000 | tf_op jit(solution)/shard_map/outputs/pallas_call | solution.py:86
  40.6 1.3 %collective-permute-done.15.k2_ref = bf16[128,1024]{1,0:T(8,128)(2,1)S(1)} collective-permute-done((bf16[128,1024]{1,0:T(8,128)(2,1)S(1)}, bf16[128,1024]{1,0:T(8,128)(2,1)S(1)}, u32[]{:S(2)}, u32[]{:S(2)}) %collective-permute-start.15) | collective-permute-done | bytes 262176 | tf_op jit(solution)/shard_map/ppermute | solution.py:27
  41.8 2.7 %collective-permute-start.16 = (f32[2,128]{1,0:T(2,128)S(1)}, f32[2,128]{1,0:T(2,128)S(1)}, u32[]{:S(2)}, u32[]{:S(2)}) collective-permute-start(f32[2,128]{1,0:T(2,128)S(1)} %add.15.own_ref), channel_id=1, source_target_pairs={{0,4},{1,5},{2,6},{3,7},{4,0},{5,1},{6,2},{7,3},{8,12},{9,13},{10,... | collective-permute-start | bytes 3080 | tf_op jit(solution)/shard_map/ppermute | solution.py:288
  44.6 1.4 %finish.1 = (bf16[128,1024]{1,0:T(8,128)(2,1)}, bf16[128,1024]{1,0:T(8,128)(2,1)}) custom-call(f32[128,1024]{1,0:T(8,128)S(1)} %get-tuple-element.69.dy_ref, f32[128,1024]{1,0:T(8,128)S(1)} %get-tuple-element.70.dv_ref, bf16[128,512]{1,0:T(8,128)(2,1)S(1)} %collective-permute-done.9.refs_0_.k1a_ref, ...), custom_call_target="tpu_custom_call" | custom-call | flops 1000000 | bytes 100000 | tf_op jit(solution)/shard_map/finish/pallas_call | solution.py:86
  46.3 0.8 %share.1 = f32[1,64]{1,0:T(1,128)} custom-call(f32[2,128]{1,0:T(2,128)S(1)} %add.15.own_ref, f32[2,128]{1,0:T(2,128)S(1)} %collective-permute-done.16.other_ref), custom_call_target="tpu_custom_call" | custom-call | flops 1000000 | bytes 100000 | tf_op jit(solution)/shard_map/share/pallas_call | solution.py:86
  (41 shorter events, 3.1 us)
Async XLA Ops:
  0.6 12.6 %collective-permute-start.1 = (bf16[1,128,1024]{2,1,0:T(8,128)(2,1)}, bf16[1,128,1024]{2,1,0:T(8,128)(2,1)S(1)}, u32[]{:S(2)}, u32[]{:S(2)}) collective-permute-start(bf16[1,128,1024]{2,1,0:T(8,128)(2,1)} %param.7), channel_id=1, source_target_pairs={{0,1},{1,0},{2,3},{3,2},{4,5},{5,4},{6,7},{7,6},{8,9},{9,8},{10,11... | collective-permute-start | bytes 786440 | tf_op jit(solution)/shard_map/ppermute | solution.py:36
  1.2 11.5 %collective-permute-start = (bf16[1,128,1024]{2,1,0:T(8,128)(2,1)}, bf16[1,128,1024]{2,1,0:T(8,128)(2,1)S(1)}, u32[]{:S(2)}, u32[]{:S(2)}) collective-permute-start(bf16[1,128,1024]{2,1,0:T(8,128)(2,1)} %param.7), channel_id=1, source_target_pairs={{0,2},{1,3},{2,4},{3,5},{4,6},{5,7},{8,10},{9,11},{10,12},{11,13},... | collective-permute-start | bytes 786440 | tf_op jit(solution)/shard_map/ppermute | solution.py:27
  5.7 13.4 %collective-permute-start.5 = (bf16[1,128,1024]{2,1,0:T(8,128)(2,1)}, bf16[1,128,1024]{2,1,0:T(8,128)(2,1)S(1)}, u32[]{:S(2)}, u32[]{:S(2)}) collective-permute-start(bf16[1,128,1024]{2,1,0:T(8,128)(2,1)} %param.8), channel_id=1, source_target_pairs={{0,2},{1,3},{2,4},{3,5},{4,6},{5,7},{6,0},{7,1},{8,10},{9,11},{10,... | collective-permute-start | bytes 786440 | tf_op jit(solution)/shard_map/ppermute | solution.py:32
  7.4 1.0 %copy-start.2 = (bf16[1,128,2048]{2,1,0:T(8,128)(2,1)S(1)}, bf16[1,128,2048]{2,1,0:T(8,128)(2,1)}, u32[]{:S(2)}) copy-start(bf16[1,128,2048]{2,1,0:T(8,128)(2,1)} %param.6) | copy-start | bytes 1572868
  7.4 1.1 %copy-start.3 = (bf16[1,128,1024]{2,1,0:T(8,128)(2,1)S(1)}, bf16[1,128,1024]{2,1,0:T(8,128)(2,1)}, u32[]{:S(2)}) copy-start(bf16[1,128,1024]{2,1,0:T(8,128)(2,1)} %param.7) | copy-start | bytes 786436
  7.4 1.1 %copy-start.4 = (f32[128]{0:T(128)S(1)}, f32[128]{0:T(128)}, u32[]{:S(2)}) copy-start(f32[128]{0:T(128)} %param.11) | copy-start | bytes 1540
  7.5 1.1 %copy-start.5 = (f32[128]{0:T(128)S(1)}, f32[128]{0:T(128)}, u32[]{:S(2)}) copy-start(f32[128]{0:T(128)} %param.10) | copy-start | bytes 1540
  7.5 6.8 %copy-start = (bf16[1,128,2048]{2,1,0:T(8,128)(2,1)S(1)}, bf16[1,128,2048]{2,1,0:T(8,128)(2,1)}, u32[]{:S(2)}) copy-start(bf16[1,128,2048]{2,1,0:T(8,128)(2,1)} %param.9) | copy-start | bytes 1572868
  8.2 11.2 %copy-start.1 = (bf16[1,128,1024]{2,1,0:T(8,128)(2,1)S(1)}, bf16[1,128,1024]{2,1,0:T(8,128)(2,1)}, u32[]{:S(2)}) copy-start(bf16[1,128,1024]{2,1,0:T(8,128)(2,1)} %param.8) | copy-start | bytes 786436
  12.7 1.4 %collective-permute-start.3 = (bf16[128,512]{1,0:T(8,128)(2,1)S(1)}, bf16[128,512]{1,0:T(8,128)(2,1)S(1)}, u32[]{:S(2)}, u32[]{:S(2)}) collective-permute-start(bf16[128,512]{1,0:T(8,128)(2,1)S(1)} %get-tuple-element.77), channel_id=1, source_target_pairs={{0,1},{1,0},{2,3},{3,2},{4,5},{5,4},{6,7},{7,6},{8,9},{9,8},{10,11... | collective-permute-start | bytes 393224 | tf_op jit(solution)/shard_map/ppermute | solution.py:36
  12.8 1.5 %collective-permute-start.2 = (bf16[128,512]{1,0:T(8,128)(2,1)S(1)}, bf16[128,512]{1,0:T(8,128)(2,1)S(1)}, u32[]{:S(2)}, u32[]{:S(2)}) collective-permute-start(bf16[128,512]{1,0:T(8,128)(2,1)S(1)} %get-tuple-element.78), channel_id=1, source_target_pairs={{0,1},{1,0},{2,3},{3,2},{4,5},{5,4},{6,7},{7,6},{8,9},{9,8},{10,11... | collective-permute-start | bytes 393224 | tf_op jit(solution)/shard_map/ppermute | solution.py:36
  19.1 1.6 %collective-permute-start.11 = (bf16[128,1024]{1,0:T(8,128)(2,1)S(1)}, bf16[128,1024]{1,0:T(8,128)(2,1)S(1)}, u32[]{:S(2)}, u32[]{:S(2)}) collective-permute-start(bf16[128,1024]{1,0:T(8,128)(2,1)S(1)} %get-tuple-element.58), channel_id=1, source_target_pairs={{0,1},{1,0},{2,3},{3,2},{4,5},{5,4},{6,7},{7,6},{8,9},{9,8},{10,11... | collective-permute-start | bytes 786440 | tf_op jit(solution)/shard_map/ppermute | solution.py:36
  19.5 2.6 %collective-permute-start.4 = (bf16[1,128,1024]{2,1,0:T(8,128)(2,1)S(1)}, bf16[1,128,1024]{2,1,0:T(8,128)(2,1)S(1)}, u32[]{:S(2)}, u32[]{:S(2)}) collective-permute-start(bf16[1,128,1024]{2,1,0:T(8,128)(2,1)S(1)} %copy-done.1), channel_id=1, source_target_pairs={{0,1},{1,0},{2,3},{3,2},{4,5},{5,4},{6,7},{7,6},{8,9},{9,8},{10,11... | collective-permute-start | bytes 786440 | tf_op jit(solution)/shard_map/ppermute | solution.py:36
  19.7 2.4 %collective-permute-start.6 = (bf16[1,128,1024]{2,1,0:T(8,128)(2,1)S(1)}, bf16[1,128,1024]{2,1,0:T(8,128)(2,1)S(1)}, u32[]{:S(2)}, u32[]{:S(2)}) collective-permute-start(bf16[1,128,1024]{2,1,0:T(8,128)(2,1)S(1)} %collective-permute-done.5), channel_id=1, source_target_pairs={{0,1},{1,0},{2,3},{3,2},{4,5},{5,4},{6,7},{7,6},{8,9},{9,8},{10,11... | collective-permute-start | bytes 786440 | tf_op jit(solution)/shard_map/ppermute | solution.py:36
  20.8 11.2 %collective-permute-start.12 = (bf16[128,1024]{1,0:T(8,128)(2,1)S(1)}, bf16[128,1024]{1,0:T(8,128)(2,1)S(1)}, u32[]{:S(2)}, u32[]{:S(2)}) collective-permute-start(bf16[128,1024]{1,0:T(8,128)(2,1)S(1)} %merge_v.1), channel_id=1, source_target_pairs={{2,0},{3,1},{4,2},{5,3},{6,4},{7,5},{10,8},{11,9},{12,10},{13,11},... | collective-permute-start | bytes 786440 | tf_op jit(solution)/shard_map/ppermute | solution.py:27
  25.2 6.7 %collective-permute-start.9 = (bf16[128,512]{1,0:T(8,128)(2,1)S(1)}, bf16[128,512]{1,0:T(8,128)(2,1)S(1)}, u32[]{:S(2)}, u32[]{:S(2)}) collective-permute-start(bf16[128,512]{1,0:T(8,128)(2,1)S(1)} %get-tuple-element.55), channel_id=1, source_target_pairs={{0,1},{1,0},{2,3},{3,2},{4,5},{5,4},{6,7},{7,6},{8,9},{9,8},{10,11... | collective-permute-start | bytes 393224 | tf_op jit(solution)/shard_map/ppermute | solution.py:36
  25.6 6.3 %collective-permute-start.10 = (bf16[128,512]{1,0:T(8,128)(2,1)S(1)}, bf16[128,512]{1,0:T(8,128)(2,1)S(1)}, u32[]{:S(2)}, u32[]{:S(2)}) collective-permute-start(bf16[128,512]{1,0:T(8,128)(2,1)S(1)} %get-tuple-element.56), channel_id=1, source_target_pairs={{0,1},{1,0},{2,3},{3,2},{4,5},{5,4},{6,7},{7,6},{8,9},{9,8},{10,11... | collective-permute-start | bytes 393224 | tf_op jit(solution)/shard_map/ppermute | solution.py:36
  25.8 1.2 %collective-permute-start.7 = (f32[2,128]{1,0:T(2,128)S(1)}, f32[2,128]{1,0:T(2,128)S(1)}, u32[]{:S(2)}, u32[]{:S(2)}) collective-permute-start(f32[2,128]{1,0:T(2,128)S(1)} %get-tuple-element.54), channel_id=1, source_target_pairs={{0,1},{1,0},{2,3},{3,2},{4,5},{5,4},{6,7},{7,6},{8,9},{9,8},{10,11... | collective-permute-start | bytes 3080 | tf_op jit(solution)/shard_map/ppermute | solution.py:288
  27.0 4.9 %collective-permute-start.8 = (f32[2,128]{1,0:T(2,128)S(1)}, f32[2,128]{1,0:T(2,128)S(1)}, u32[]{:S(2)}, u32[]{:S(2)}) collective-permute-start(f32[2,128]{1,0:T(2,128)S(1)} %add.12), channel_id=1, source_target_pairs={{0,2},{1,3},{2,0},{3,1},{4,6},{5,7},{6,4},{7,5},{8,10},{9,11},{10,... | collective-permute-start | bytes 3080 | tf_op jit(solution)/shard_map/ppermute | solution.py:288
  32.0 9.8 %collective-permute-start.15 = (bf16[128,1024]{1,0:T(8,128)(2,1)S(1)}, bf16[128,1024]{1,0:T(8,128)(2,1)S(1)}, u32[]{:S(2)}, u32[]{:S(2)}) collective-permute-start(bf16[128,1024]{1,0:T(8,128)(2,1)S(1)} %merge_k.1), channel_id=1, source_target_pairs={{2,0},{3,1},{4,2},{5,3},{6,4},{7,5},{10,8},{11,9},{12,10},{13,11},... | collective-permute-start | bytes 786440 | tf_op jit(solution)/shard_map/ppermute | solution.py:27
  33.3 3.6 %collective-permute-start.13 = (f32[2,128]{1,0:T(2,128)S(1)}, f32[2,128]{1,0:T(2,128)S(1)}, u32[]{:S(2)}, u32[]{:S(2)}) collective-permute-start(f32[2,128]{1,0:T(2,128)S(1)} %add.13), channel_id=1, source_target_pairs={{0,8},{8,0},{16,24},{24,16},{1,9},{9,1},{17,25},{25,17},{2,10},{10... | collective-permute-start | bytes 3080 | tf_op jit(solution)/shard_map/ppermute | solution.py:288
  37.0 3.6 %collective-permute-start.14 = (f32[2,128]{1,0:T(2,128)S(1)}, f32[2,128]{1,0:T(2,128)S(1)}, u32[]{:S(2)}, u32[]{:S(2)}) collective-permute-start(f32[2,128]{1,0:T(2,128)S(1)} %add.14), channel_id=1, source_target_pairs={{0,16},{8,24},{16,0},{24,8},{1,17},{9,25},{17,1},{25,9},{2,18},{10... | collective-permute-start | bytes 3080 | tf_op jit(solution)/shard_map/ppermute | solution.py:288
  41.8 4.5 %collective-permute-start.16 = (f32[2,128]{1,0:T(2,128)S(1)}, f32[2,128]{1,0:T(2,128)S(1)}, u32[]{:S(2)}, u32[]{:S(2)}) collective-permute-start(f32[2,128]{1,0:T(2,128)S(1)} %add.15.own_ref), channel_id=1, source_target_pairs={{0,4},{1,5},{2,6},{3,7},{4,0},{5,1},{6,2},{7,3},{8,12},{9,13},{10,... | collective-permute-start | bytes 3080 | tf_op jit(solution)/shard_map/ppermute | solution.py:288

commit v4 on v3

--- a/solution.py
+++ b/solution.py
@@ -60,11 +60,6 @@
     return rotated, dot(rotated, swap).astype(BF16), x * inverse, inverse
 
 
-def norm_back(d_y, normed, inverse, gain):
-    d_normed = d_y * gain
-    return inverse * (d_normed - normed * row_mean(d_normed * normed))
-
-
 def fold(x):
     return jnp.sum(x.reshape(-1, 8, x.shape[-1]), axis=0)
 
@@ -77,9 +72,13 @@
     return jnp.concatenate([ref[:, columns(GROUP * h + j, head)] for j in range(GROUP)], axis=0)
 
 
-def each_head(count, body):
-    for h in range(count):
-        body(h)
+def each_head(count, *stages):
+    held = {}
+    for step in range(count + len(stages) - 1):
+        for i, stage in enumerate(stages):
+            h = step - i
+            if 0 <= h < count:
+                held[h] = stage(h, *held.pop(h, ())) or ()
 
 
 def call(kernel, name, outs, args, flops=1_000_000, traffic=100_000, scratch=()):
@@ -155,27 +154,39 @@
     bias = jnp.where((key > row) & (key <= row + far) & (key >= start), 0.0, HIDDEN)
     bias = jnp.concatenate([bias] * GROUP, axis=1)
 
-    def body(h):
+    def first(h):
         cols = columns(h, head)
         half_ref, low = (k1b_ref, h) if h < heads // 2 else (k1c_ref, h - heads // 2)
         near = jnp.where(odd, k1a_ref[:, cols], half_ref[:, columns(low, head)])
         raw = jnp.concatenate([k2_ref[:, cols], near], axis=0)
-        rotated, swapped, normed, _ = norm_rotate(raw, turn, turn_s, swap)
+        x = raw.astype(F32)
+        return raw, row_mean(x * x), dot(raw, swap)
+
+    def second(h, raw, mean_sq, other):
+        x = raw.astype(F32)
+        inverse = lax.rsqrt(mean_sq + EPSILON)
+        rotated = (inverse * (x * turn + other * turn_s)).astype(BF16)
         keys_ref[h, :, :head] = rotated
-        keys_ref[h, :, head:] = swapped
-        unit_ref[h] = normed
+        unit_ref[h] = x * inverse
         keys = jnp.concatenate([rotated, own_ref[h, :, :head]], axis=0)
-        scores = dot(keys, q_ref[h, :, :head], ((1,), (1,))) + bias
+        return rotated, dot(keys, q_ref[h, :, :head], ((1,), (1,))) + bias
+
+    def third(h, rotated, scores):
+        keys_ref[h, :, head:] = dot(rotated, swap).astype(BF16)
         top = jnp.max(scores, axis=0, keepdims=True)
         exps = jnp.exp2((scores - top) * LOG2_SCALE)
         probs = exps * (1.0 / jnp.sum(exps, axis=0, keepdims=True))
         probs_ref[h] = probs
+        return (probs,)
+
+    def fourth(h, probs):
+        cols = columns(h, head)
         d_value = dot(probs.astype(BF16), stacked(do_ref, h, head))
         dv2_ref[:, cols] = d_value[: far - rows].astype(BF16)
         dv1_ref[:, cols] = d_value[far - rows : far].astype(BF16)
         dv_ref[:, cols] = d_value[far:]
 
-    each_head(heads, body)
+    each_head(heads, first, second, third, fourth)
 
 
 def grads_kernel(
@@ -192,17 +203,24 @@
     q_sin = jnp.concatenate([sine[far:]] * GROUP, axis=0)
     dg_ref[...] = jnp.zeros_like(dg_ref)
 
-    def body(h):
+    def first(h):
         cols = columns(h, head)
         values = jnp.concatenate([v2_ref[:, cols], jnp.where(odd, v1a_ref[:, cols], v1b_ref[:, cols]), v0_ref[:, cols]], axis=0)
         grad_out = stacked(do_ref, h, head)
+        return (dot(values, grad_out, ((1,), (1,))),)
+
+    def second(h, d_prob):
         probs = probs_ref[h]
-        d_prob = dot(values, grad_out, ((1,), (1,)))
         delta = jnp.sum(probs * d_prob, axis=0, keepdims=True)
-        d_score = (probs * (d_prob - delta) * SCORE_SCALE).astype(BF16)
+        return ((probs * (d_prob - delta) * SCORE_SCALE).astype(BF16),)
+
+    def third(h, d_score):
         d_key = dot(d_score, q_ref[h])
         d_query = dot(d_score, jnp.concatenate([keys_ref[h], own_ref[h]], axis=0), ((0,), (0,)))
-
+        return d_key, d_query
+
+    def fourth(h, d_key, d_query):
+        cols = columns(h, head)
         dk2_ref[:, cols] = d_key[: far - rows, :head].astype(BF16)
         dk1_ref, low = (dk1a_ref, h) if h < heads // 2 else (dk1b_ref, h - heads // 2)
         dk1_ref[:, columns(low, head)] = d_key[far - rows : far, :head].astype(BF16)
@@ -216,7 +234,7 @@
         dqy_ref[h] = d_y
         dg_ref[0:8, :] += fold(d_y * q_unit_ref[h])
 
-    each_head(heads, body)
+    each_head(heads, first, second, third, fourth)
     sum_ref[0:1] = jnp.sum(dg_ref[0:8], axis=0, keepdims=True)
     sum_ref[1:2] = jnp.sum(dg_ref[8:16], axis=0, keepdims=True)
 
@@ -227,17 +245,21 @@
     odd = lax.rem(lax.axis_index("ctx"), 2) == 1
     q_gain = gain_ref[...]
 
-    def body(h):
+    def first(h):
         cols = columns(h, head)
         values = jnp.concatenate([v2_ref[:, cols], jnp.where(odd, v1a_ref[:, cols], v1b_ref[:, cols]), v0_ref[:, cols]], axis=0)
-        result = dot(probs_ref[h].astype(BF16), values, ((0,), (0,))).astype(BF16)
-        d_q = norm_back(dqy_ref[h], q_unit_ref[h], q_inv_ref[h], q_gain).astype(BF16)
+        d_normed = dqy_ref[h] * q_gain
+        return dot(probs_ref[h].astype(BF16), values, ((0,), (0,))), d_normed, row_mean(d_normed * q_unit_ref[h])
+
+    def second(h, result, d_normed, mean):
+        d_q = (q_inv_ref[h] * (d_normed - q_unit_ref[h] * mean)).astype(BF16)
+        result = result.astype(BF16)
         for j in range(GROUP):
             wide = columns(GROUP * h + j, head)
             out_ref[:, wide] = result[j * rows : (j + 1) * rows]
             dq_ref[:, wide] = d_q[j * rows : (j + 1) * rows]
 
-    each_head(heads, body)
+    each_head(heads, first, second)
 
 
 def merge_kernel(far_ref, *refs):
@@ -260,18 +282,24 @@
     cosine, sine = angle_ref[0, far:], angle_ref[1, far:]
     gain = gain_ref[...]
 
-    def body(h):
+    def first(h):
         cols = columns(h, head)
         near = jnp.where(odd, 0.0, v1_ref[:, cols].astype(F32))
         dv_out[:, cols] = (dv_ref[:, cols] + near + v2_ref[:, cols].astype(F32)).astype(BF16)
         k1_ref, low = (k1a_ref, h) if h < heads // 2 else (k1b_ref, h - heads // 2)
         near = jnp.where(odd, 0.0, k1_ref[:, columns(low, head)].astype(F32))
         rest = k2_ref[:, cols]
-        swapped = dot(jnp.concatenate([near.astype(BF16), rest], axis=1), swaps)
-        d_y = dy_ref[:, cols] + ((near + rest.astype(F32)) * cosine - swapped * sine)
-        dk_out[:, cols] = norm_back(d_y, unit_ref[h], inv_ref[h], gain).astype(BF16)
-
-    each_head(heads, body)
+        return near + rest.astype(F32), dot(jnp.concatenate([near.astype(BF16), rest], axis=1), swaps)
+
+    def second(h, both, swapped):
+        d_y = dy_ref[:, columns(h, head)] + (both * cosine - swapped * sine)
+        d_normed = d_y * gain
+        return d_normed, row_mean(d_normed * unit_ref[h])
+
+    def third(h, d_normed, mean):
+        dk_out[:, columns(h, head)] = (inv_ref[h] * (d_normed - unit_ref[h] * mean)).astype(BF16)
+
+    each_head(heads, first, second, third)
 
 
 def share_kernel(own_ref, other_ref, out_ref):

time: 47.3 us -> 45.6 us (0.964)
  Pallas kernels: 15.6 us -> 13 us
  waiting for transfers between devices: 9.83 us -> 11.4 us
  starting transfers between devices: 20.4 us -> 19.8 us
    pallas_call x9, Pallas kernels: 15.6 us -> 13 us  [call(): pl.pallas_call(kernel, name=name, in_specs=[IN_VMEM] * len(args), out_spe...]
    ppermute x5, waiting for transfers between devices: 5.24 us -> 6.18 us  [all_sum_term(): lax.ppermute(value, axis, [(i, i ^ step) for i in range(lax.axis_size(axi...]
    ppermute x1, waiting for transfers between devices: 0.01 us -> 0.49 us  [ring_hop(): lax.ppermute(value, 'ctx', [(i, (i + steps) % count) for i in range(count)])]
  transfers between devices with their start and end apart: 17 -> 17, of which waited for: 9 -> 10; matrix products, arithmetic and copies ran while one was open for 0% -> 0% of each run, Pallas kernels for 31% -> 27%
where the time goes in v4:
time: 45.6 us; the launch traced here: 45.4 us
  starting transfers between devices  19.8 us (43%)
  Pallas kernels  13 us (29%)
  waiting for transfers between devices  11.4 us (25%)
  between operations  0.79 us (2%)
    pallas_call x9, Pallas kernels, call(): pl.pallas_call(kernel, name=name, in_specs=[IN_VMEM] * len(args), out_spe...  13 us
    ppermute x5, starting transfers between devices, all_sum_term(): lax.ppermute(value, axis, [(i, i ^ step) for i in range(lax.axis_size(axi...  8.87 us
    ppermute x3, starting transfers between devices, hop(): lax.ppermute(value, 'ctx', [(i, i + steps) for i in range(initial, last)])  7.08 us
    ppermute x5, waiting for transfers between devices, all_sum_term(): lax.ppermute(value, axis, [(i, i ^ step) for i in range(lax.axis_size(axi...  6.18 us
    ppermute x3, waiting for transfers between devices, hop(): lax.ppermute(value, 'ctx', [(i, i + steps) for i in range(initial, last)])  2.67 us
    ppermute x8, starting transfers between devices, swap_pairs(): lax.ppermute(value, 'ctx', [(i, i ^ 1) for i in range(lax.axis_size('ctx'...  2.21 us
    ppermute x8, waiting for transfers between devices, swap_pairs(): lax.ppermute(value, 'ctx', [(i, i ^ 1) for i in range(lax.axis_size('ctx'...  2.05 us
    ppermute x1, starting transfers between devices, ring_hop(): lax.ppermute(value, 'ctx', [(i, (i + steps) % count) for i in range(count)])  1.62 us
  transfers between devices with their start and end apart: 17, of which 10 were waited for; matrix products, arithmetic and copies ran while one was open for 0% of the time, Pallas kernels for 27%

profile of v4, /device:TPU:0, one launch (start us, length us, event | category | flops | bytes accessed | tf_op | source)
XLA Modules:
  0.0 45.4 jit_solution(2044073090039565278)
XLA Ops:
  0.6 0.6 %collective-permute-start.1 = (bf16[1,128,1024]{2,1,0:T(8,128)(2,1)}, bf16[1,128,1024]{2,1,0:T(8,128)(2,1)S(1)}, u32[]{:S(2)}, u32[]{:S(2)}) collective-permute-start(bf16[1,128,1024]{2,1,0:T(8,128)(2,1)} %param.7), channel_id=1, source_target_pairs={{0,1},{1,0},{2,3},{3,2},{4,5},{5,4},{6,7},{7,6},{8,9},{9,8},{10,11... | collective-permute-start | bytes 786440 | tf_op jit(solution)/shard_map/ppermute | solution.py:36
  1.2 4.5 %collective-permute-start = (bf16[1,128,1024]{2,1,0:T(8,128)(2,1)}, bf16[1,128,1024]{2,1,0:T(8,128)(2,1)S(1)}, u32[]{:S(2)}, u32[]{:S(2)}) collective-permute-start(bf16[1,128,1024]{2,1,0:T(8,128)(2,1)} %param.7), channel_id=1, source_target_pairs={{0,2},{1,3},{2,4},{3,5},{4,6},{5,7},{8,10},{9,11},{10,12},{11,13},... | collective-permute-start | bytes 786440 | tf_op jit(solution)/shard_map/ppermute | solution.py:27
  5.7 1.6 %collective-permute-start.5 = (bf16[1,128,1024]{2,1,0:T(8,128)(2,1)}, bf16[1,128,1024]{2,1,0:T(8,128)(2,1)S(1)}, u32[]{:S(2)}, u32[]{:S(2)}) collective-permute-start(bf16[1,128,1024]{2,1,0:T(8,128)(2,1)} %param.8), channel_id=1, source_target_pairs={{0,2},{1,3},{2,4},{3,5},{4,6},{5,7},{6,0},{7,1},{8,10},{9,11},{10,... | collective-permute-start | bytes 786440 | tf_op jit(solution)/shard_map/ppermute | solution.py:32
  7.5 0.7 %tables.1.angle_ref = f32[2,384,128]{2,1,0:T(8,128)S(1)} custom-call(f32[2,128]{1,0:T(2,128)S(1)} %pad_maximum_fusion.freq_ref), custom_call_target="tpu_custom_call" | custom-call | flops 10000000000 | bytes 100000 | tf_op jit(solution)/shard_map/tables/pallas_call | solution.py:85
  8.5 2.6 %prepare.1 = (bf16[8,256,256]{2,1,0:T(8,128)(2,1)S(1)}, f32[8,256,128]{2,1,0:T(8,128)S(1)}, f32[8,256,128]{2,1,0:T(8,128)S(1)}, bf16[8,128,256]{2,1,0:T(8,128)(2...) custom-call(bf16[128,2048]{1,0:T(8,128)(2,1)S(1)} %bitcast.31, ...), custom_call_target="tpu_custom_call" | custom-call | flops 1000000 | bytes 100000 | tf_op jit(solution)/shard_map/prepare/pallas_call | solution.py:85
  11.1 1.6 %collective-permute-done = bf16[1,128,1024]{2,1,0:T(8,128)(2,1)S(1)} collective-permute-done((bf16[1,128,1024]{2,1,0:T(8,128)(2,1)}, bf16[1,128,1024]{2,1,0:T(8,128)(2,1)S(1)}, u32[]{:S(2)}, u32[]{:S(2)}) %collective-permute-start) | collective-permute-done | bytes 262176 | tf_op jit(solution)/shard_map/ppermute | solution.py:27
  13.3 0.8 %collective-permute-done.3.k1c_ref = bf16[128,512]{1,0:T(8,128)(2,1)S(1)} collective-permute-done((bf16[128,512]{1,0:T(8,128)(2,1)S(1)}, bf16[128,512]{1,0:T(8,128)(2,1)S(1)}, u32[]{:S(2)}, u32[]{:S(2)}) %collective-permute-start.3) | collective-permute-done | bytes 131104 | tf_op jit(solution)/shard_map/ppermute | solution.py:36
  14.3 3.0 %scores.1 = (f32[8,384,256]{2,1,0:T(8,128)S(1)}, bf16[8,256,256]{2,1,0:T(8,128)(2,1)S(1)}, f32[8,256,128]{2,1,0:T(8,128)S(1)}, f32[128,1024]{1,0:T(8,128)S(1)}, ...) custom-call(bf16[8,256,256]{2,1,0:T(8,128)(2,1)S(1)} %get-tuple-element.42.q_ref, ...), custom_call_target="tpu_custom_call" | custom-call | flops 1000000 | bytes 100000 | tf_op jit(solution)/shard_map/scores/pallas_call | solution.py:85
  17.8 0.5 %collective-permute-start.4 = (bf16[1,128,1024]{2,1,0:T(8,128)(2,1)S(1)}, bf16[1,128,1024]{2,1,0:T(8,128)(2,1)S(1)}, u32[]{:S(2)}, u32[]{:S(2)}) collective-permute-start(bf16[1,128,1024]{2,1,0:T(8,128)(2,1)S(1)} %copy-done.1), channel_id=1, source_target_pairs={{0,1},{1,0},{2,3},{3,2},{4,5},{5,4},{6,7},{7,6},{8,9},{9,8},{10,11... | collective-permute-start | bytes 786440 | tf_op jit(solution)/shard_map/ppermute | solution.py:36
  18.3 1.0 %collective-permute-done.11.refs_0_.v1_ref = bf16[128,1024]{1,0:T(8,128)(2,1)S(1)} collective-permute-done((bf16[128,1024]{1,0:T(8,128)(2,1)S(1)}, bf16[128,1024]{1,0:T(8,128)(2,1)S(1)}, u32[]{:S(2)}, u32[]{:S(2)}) %collective-permute-start.11) | collective-permute-done | bytes 262176 | tf_op jit(solution)/shard_map/ppermute | solution.py:36
  19.4 1.3 %collective-permute-start.12 = (bf16[128,1024]{1,0:T(8,128)(2,1)S(1)}, bf16[128,1024]{1,0:T(8,128)(2,1)S(1)}, u32[]{:S(2)}, u32[]{:S(2)}) collective-permute-start(bf16[128,1024]{1,0:T(8,128)(2,1)S(1)} %merge_v.1), channel_id=1, source_target_pairs={{2,0},{3,1},{4,2},{5,3},{6,4},{7,5},{10,8},{11,9},{12,10},{13,11},... | collective-permute-start | bytes 786440 | tf_op jit(solution)/shard_map/ppermute | solution.py:27
  20.8 2.3 %grads.1 = (f32[8,256,128]{2,1,0:T(8,128)S(1)}, f32[128,1024]{1,0:T(8,128)S(1)}, bf16[128,512]{1,0:T(8,128)(2,1)S(1)}, bf16[128,512]{1,0:T(8,128)(2,1)S(1)}, bf1...) custom-call(f32[8,384,256]{2,1,0:T(8,128)S(1)} %get-tuple-element.46.probs_ref, ...), custom_call_target="tpu_custom_call" | custom-call | flops 1000000 | bytes 100000 | tf_op jit(solution)/shard_map/grads/pallas_call | solution.py:85
  23.7 1.0 %collective-permute-done.7 = f32[2,128]{1,0:T(2,128)S(1)} collective-permute-done((f32[2,128]{1,0:T(2,128)S(1)}, f32[2,128]{1,0:T(2,128)S(1)}, u32[]{:S(2)}, u32[]{:S(2)}) %collective-permute-start.7) | collective-permute-done | bytes 1056 | tf_op jit(solution)/shard_map/ppermute | solution.py:316
  24.8 3.0 %collective-permute-start.8 = (f32[2,128]{1,0:T(2,128)S(1)}, f32[2,128]{1,0:T(2,128)S(1)}, u32[]{:S(2)}, u32[]{:S(2)}) collective-permute-start(f32[2,128]{1,0:T(2,128)S(1)} %add.12), channel_id=1, source_target_pairs={{0,2},{1,3},{2,0},{3,1},{4,6},{5,7},{6,4},{7,5},{8,10},{9,11},{10,... | collective-permute-start | bytes 3080 | tf_op jit(solution)/shard_map/ppermute | solution.py:316
  27.8 2.6 %collective-permute-done.8 = f32[2,128]{1,0:T(2,128)S(1)} collective-permute-done((f32[2,128]{1,0:T(2,128)S(1)}, f32[2,128]{1,0:T(2,128)S(1)}, u32[]{:S(2)}, u32[]{:S(2)}) %collective-permute-start.8) | collective-permute-done | bytes 1056 | tf_op jit(solution)/shard_map/ppermute | solution.py:316
  30.5 1.3 %collective-permute-start.15 = (bf16[128,1024]{1,0:T(8,128)(2,1)S(1)}, bf16[128,1024]{1,0:T(8,128)(2,1)S(1)}, u32[]{:S(2)}, u32[]{:S(2)}) collective-permute-start(bf16[128,1024]{1,0:T(8,128)(2,1)S(1)} %merge_k.1), channel_id=1, source_target_pairs={{2,0},{3,1},{4,2},{5,3},{6,4},{7,5},{10,8},{11,9},{12,10},{13,11},... | collective-permute-start | bytes 786440 | tf_op jit(solution)/shard_map/ppermute | solution.py:27
  31.8 1.6 %collective-permute-start.13 = (f32[2,128]{1,0:T(2,128)S(1)}, f32[2,128]{1,0:T(2,128)S(1)}, u32[]{:S(2)}, u32[]{:S(2)}) collective-permute-start(f32[2,128]{1,0:T(2,128)S(1)} %add.13), channel_id=1, source_target_pairs={{0,8},{8,0},{16,24},{24,16},{1,9},{9,1},{17,25},{25,17},{2,10},{10... | collective-permute-start | bytes 3080 | tf_op jit(solution)/shard_map/ppermute | solution.py:316
  33.4 2.1 %collective-permute-done.13 = f32[2,128]{1,0:T(2,128)S(1)} collective-permute-done((f32[2,128]{1,0:T(2,128)S(1)}, f32[2,128]{1,0:T(2,128)S(1)}, u32[]{:S(2)}, u32[]{:S(2)}) %collective-permute-start.13) | collective-permute-done | bytes 1056 | tf_op jit(solution)/shard_map/ppermute | solution.py:316
  35.5 1.5 %collective-permute-start.14 = (f32[2,128]{1,0:T(2,128)S(1)}, f32[2,128]{1,0:T(2,128)S(1)}, u32[]{:S(2)}, u32[]{:S(2)}) collective-permute-start(f32[2,128]{1,0:T(2,128)S(1)} %add.14), channel_id=1, source_target_pairs={{0,16},{8,24},{16,0},{24,8},{1,17},{9,25},{17,1},{25,9},{2,18},{10... | collective-permute-start | bytes 3080 | tf_op jit(solution)/shard_map/ppermute | solution.py:316
  37.0 2.0 %outputs.1 = (bf16[128,2048]{1,0:T(8,128)(2,1)}, bf16[128,2048]{1,0:T(8,128)(2,1)}) custom-call(f32[8,384,256]{2,1,0:T(8,128)S(1)} %get-tuple-element.46.probs_ref, bf16[128,1024]{1,0:T(8,128)(2,1)S(1)} %bitcast.24, bf16[128,1024]{1,0:T(8,128)(2,1)S(1)} %bitcast.28, bf16[128,1024]{1,0:T(8,128)(2,1)S(1)} %bitcast.30, bf16[128,1024]{1,0:T(8,128)(2,1)S(1)} %bitcast.26, ...), custom_call_target="tpu_custom_call" | custom-call | flops 1000000 | bytes 100000 | tf_op jit(solution)/shard_map/outputs/pallas_call | solution.py:85
  39.0 1.1 %collective-permute-done.15.k2_ref = bf16[128,1024]{1,0:T(8,128)(2,1)S(1)} collective-permute-done((bf16[128,1024]{1,0:T(8,128)(2,1)S(1)}, bf16[128,1024]{1,0:T(8,128)(2,1)S(1)}, u32[]{:S(2)}, u32[]{:S(2)}) %collective-permute-start.15) | collective-permute-done | bytes 262176 | tf_op jit(solution)/shard_map/ppermute | solution.py:27
  40.1 2.7 %collective-permute-start.16 = (f32[2,128]{1,0:T(2,128)S(1)}, f32[2,128]{1,0:T(2,128)S(1)}, u32[]{:S(2)}, u32[]{:S(2)}) collective-permute-start(f32[2,128]{1,0:T(2,128)S(1)} %add.15.own_ref), channel_id=1, source_target_pairs={{0,4},{1,5},{2,6},{3,7},{4,0},{5,1},{6,2},{7,3},{8,12},{9,13},{10,... | collective-permute-start | bytes 3080 | tf_op jit(solution)/shard_map/ppermute | solution.py:316
  42.8 1.4 %finish.1 = (bf16[128,1024]{1,0:T(8,128)(2,1)}, bf16[128,1024]{1,0:T(8,128)(2,1)}) custom-call(f32[128,1024]{1,0:T(8,128)S(1)} %get-tuple-element.69.dy_ref, f32[128,1024]{1,0:T(8,128)S(1)} %get-tuple-element.70.dv_ref, bf16[128,512]{1,0:T(8,128)(2,1)S(1)} %collective-permute-done.9.refs_0_.k1a_ref, ...), custom_call_target="tpu_custom_call" | custom-call | flops 1000000 | bytes 100000 | tf_op jit(solution)/shard_map/finish/pallas_call | solution.py:85
  44.6 0.8 %share.1 = f32[1,64]{1,0:T(1,128)} custom-call(f32[2,128]{1,0:T(2,128)S(1)} %add.15.own_ref, f32[2,128]{1,0:T(2,128)S(1)} %collective-permute-done.16.other_ref), custom_call_target="tpu_custom_call" | custom-call | flops 1000000 | bytes 100000 | tf_op jit(solution)/shard_map/share/pallas_call | solution.py:85
  (41 shorter events, 3.1 us)
Async XLA Ops:
  0.6 12.6 %collective-permute-start.1 = (bf16[1,128,1024]{2,1,0:T(8,128)(2,1)}, bf16[1,128,1024]{2,1,0:T(8,128)(2,1)S(1)}, u32[]{:S(2)}, u32[]{:S(2)}) collective-permute-start(bf16[1,128,1024]{2,1,0:T(8,128)(2,1)} %param.7), channel_id=1, source_target_pairs={{0,1},{1,0},{2,3},{3,2},{4,5},{5,4},{6,7},{7,6},{8,9},{9,8},{10,11... | collective-permute-start | bytes 786440 | tf_op jit(solution)/shard_map/ppermute | solution.py:36
  1.2 11.5 %collective-permute-start = (bf16[1,128,1024]{2,1,0:T(8,128)(2,1)}, bf16[1,128,1024]{2,1,0:T(8,128)(2,1)S(1)}, u32[]{:S(2)}, u32[]{:S(2)}) collective-permute-start(bf16[1,128,1024]{2,1,0:T(8,128)(2,1)} %param.7), channel_id=1, source_target_pairs={{0,2},{1,3},{2,4},{3,5},{4,6},{5,7},{8,10},{9,11},{10,12},{11,13},... | collective-permute-start | bytes 786440 | tf_op jit(solution)/shard_map/ppermute | solution.py:27
  5.7 12.1 %collective-permute-start.5 = (bf16[1,128,1024]{2,1,0:T(8,128)(2,1)}, bf16[1,128,1024]{2,1,0:T(8,128)(2,1)S(1)}, u32[]{:S(2)}, u32[]{:S(2)}) collective-permute-start(bf16[1,128,1024]{2,1,0:T(8,128)(2,1)} %param.8), channel_id=1, source_target_pairs={{0,2},{1,3},{2,4},{3,5},{4,6},{5,7},{6,0},{7,1},{8,10},{9,11},{10,... | collective-permute-start | bytes 786440 | tf_op jit(solution)/shard_map/ppermute | solution.py:32
  7.4 1.0 %copy-start.2 = (bf16[1,128,2048]{2,1,0:T(8,128)(2,1)S(1)}, bf16[1,128,2048]{2,1,0:T(8,128)(2,1)}, u32[]{:S(2)}) copy-start(bf16[1,128,2048]{2,1,0:T(8,128)(2,1)} %param.6) | copy-start | bytes 1572868
  7.4 1.1 %copy-start.3 = (bf16[1,128,1024]{2,1,0:T(8,128)(2,1)S(1)}, bf16[1,128,1024]{2,1,0:T(8,128)(2,1)}, u32[]{:S(2)}) copy-start(bf16[1,128,1024]{2,1,0:T(8,128)(2,1)} %param.7) | copy-start | bytes 786436
  7.4 1.1 %copy-start.4 = (f32[128]{0:T(128)S(1)}, f32[128]{0:T(128)}, u32[]{:S(2)}) copy-start(f32[128]{0:T(128)} %param.11) | copy-start | bytes 1540
  7.5 1.1 %copy-start.5 = (f32[128]{0:T(128)S(1)}, f32[128]{0:T(128)}, u32[]{:S(2)}) copy-start(f32[128]{0:T(128)} %param.10) | copy-start | bytes 1540
  7.5 6.8 %copy-start = (bf16[1,128,2048]{2,1,0:T(8,128)(2,1)S(1)}, bf16[1,128,2048]{2,1,0:T(8,128)(2,1)}, u32[]{:S(2)}) copy-start(bf16[1,128,2048]{2,1,0:T(8,128)(2,1)} %param.9) | copy-start | bytes 1572868
  8.2 9.6 %copy-start.1 = (bf16[1,128,1024]{2,1,0:T(8,128)(2,1)S(1)}, bf16[1,128,1024]{2,1,0:T(8,128)(2,1)}, u32[]{:S(2)}) copy-start(bf16[1,128,1024]{2,1,0:T(8,128)(2,1)} %param.8) | copy-start | bytes 786436
  12.7 1.4 %collective-permute-start.3 = (bf16[128,512]{1,0:T(8,128)(2,1)S(1)}, bf16[128,512]{1,0:T(8,128)(2,1)S(1)}, u32[]{:S(2)}, u32[]{:S(2)}) collective-permute-start(bf16[128,512]{1,0:T(8,128)(2,1)S(1)} %get-tuple-element.77), channel_id=1, source_target_pairs={{0,1},{1,0},{2,3},{3,2},{4,5},{5,4},{6,7},{7,6},{8,9},{9,8},{10,11... | collective-permute-start | bytes 393224 | tf_op jit(solution)/shard_map/ppermute | solution.py:36
  12.8 1.5 %collective-permute-start.2 = (bf16[128,512]{1,0:T(8,128)(2,1)S(1)}, bf16[128,512]{1,0:T(8,128)(2,1)S(1)}, u32[]{:S(2)}, u32[]{:S(2)}) collective-permute-start(bf16[128,512]{1,0:T(8,128)(2,1)S(1)} %get-tuple-element.78), channel_id=1, source_target_pairs={{0,1},{1,0},{2,3},{3,2},{4,5},{5,4},{6,7},{7,6},{8,9},{9,8},{10,11... | collective-permute-start | bytes 393224 | tf_op jit(solution)/shard_map/ppermute | solution.py:36
  17.8 1.5 %collective-permute-start.11 = (bf16[128,1024]{1,0:T(8,128)(2,1)S(1)}, bf16[128,1024]{1,0:T(8,128)(2,1)S(1)}, u32[]{:S(2)}, u32[]{:S(2)}) collective-permute-start(bf16[128,1024]{1,0:T(8,128)(2,1)S(1)} %get-tuple-element.58), channel_id=1, source_target_pairs={{0,1},{1,0},{2,3},{3,2},{4,5},{5,4},{6,7},{7,6},{8,9},{9,8},{10,11... | collective-permute-start | bytes 786440 | tf_op jit(solution)/shard_map/ppermute | solution.py:36
  17.8 2.9 %collective-permute-start.4 = (bf16[1,128,1024]{2,1,0:T(8,128)(2,1)S(1)}, bf16[1,128,1024]{2,1,0:T(8,128)(2,1)S(1)}, u32[]{:S(2)}, u32[]{:S(2)}) collective-permute-start(bf16[1,128,1024]{2,1,0:T(8,128)(2,1)S(1)} %copy-done.1), channel_id=1, source_target_pairs={{0,1},{1,0},{2,3},{3,2},{4,5},{5,4},{6,7},{7,6},{8,9},{9,8},{10,11... | collective-permute-start | bytes 786440 | tf_op jit(solution)/shard_map/ppermute | solution.py:36
  18.3 2.4 %collective-permute-start.6 = (bf16[1,128,1024]{2,1,0:T(8,128)(2,1)S(1)}, bf16[1,128,1024]{2,1,0:T(8,128)(2,1)S(1)}, u32[]{:S(2)}, u32[]{:S(2)}) collective-permute-start(bf16[1,128,1024]{2,1,0:T(8,128)(2,1)S(1)} %collective-permute-done.5), channel_id=1, source_target_pairs={{0,1},{1,0},{2,3},{3,2},{4,5},{5,4},{6,7},{7,6},{8,9},{9,8},{10,11... | collective-permute-start | bytes 786440 | tf_op jit(solution)/shard_map/ppermute | solution.py:36
  19.4 11.0 %collective-permute-start.12 = (bf16[128,1024]{1,0:T(8,128)(2,1)S(1)}, bf16[128,1024]{1,0:T(8,128)(2,1)S(1)}, u32[]{:S(2)}, u32[]{:S(2)}) collective-permute-start(bf16[128,1024]{1,0:T(8,128)(2,1)S(1)} %merge_v.1), channel_id=1, source_target_pairs={{2,0},{3,1},{4,2},{5,3},{6,4},{7,5},{10,8},{11,9},{12,10},{13,11},... | collective-permute-start | bytes 786440 | tf_op jit(solution)/shard_map/ppermute | solution.py:27
  23.0 7.4 %collective-permute-start.9 = (bf16[128,512]{1,0:T(8,128)(2,1)S(1)}, bf16[128,512]{1,0:T(8,128)(2,1)S(1)}, u32[]{:S(2)}, u32[]{:S(2)}) collective-permute-start(bf16[128,512]{1,0:T(8,128)(2,1)S(1)} %get-tuple-element.55), channel_id=1, source_target_pairs={{0,1},{1,0},{2,3},{3,2},{4,5},{5,4},{6,7},{7,6},{8,9},{9,8},{10,11... | collective-permute-start | bytes 393224 | tf_op jit(solution)/shard_map/ppermute | solution.py:36
  23.2 7.2 %collective-permute-start.10 = (bf16[128,512]{1,0:T(8,128)(2,1)S(1)}, bf16[128,512]{1,0:T(8,128)(2,1)S(1)}, u32[]{:S(2)}, u32[]{:S(2)}) collective-permute-start(bf16[128,512]{1,0:T(8,128)(2,1)S(1)} %get-tuple-element.56), channel_id=1, source_target_pairs={{0,1},{1,0},{2,3},{3,2},{4,5},{5,4},{6,7},{7,6},{8,9},{9,8},{10,11... | collective-permute-start | bytes 393224 | tf_op jit(solution)/shard_map/ppermute | solution.py:36
  23.6 1.2 %collective-permute-start.7 = (f32[2,128]{1,0:T(2,128)S(1)}, f32[2,128]{1,0:T(2,128)S(1)}, u32[]{:S(2)}, u32[]{:S(2)}) collective-permute-start(f32[2,128]{1,0:T(2,128)S(1)} %get-tuple-element.54), channel_id=1, source_target_pairs={{0,1},{1,0},{2,3},{3,2},{4,5},{5,4},{6,7},{7,6},{8,9},{9,8},{10,11... | collective-permute-start | bytes 3080 | tf_op jit(solution)/shard_map/ppermute | solution.py:316
  24.8 5.6 %collective-permute-start.8 = (f32[2,128]{1,0:T(2,128)S(1)}, f32[2,128]{1,0:T(2,128)S(1)}, u32[]{:S(2)}, u32[]{:S(2)}) collective-permute-start(f32[2,128]{1,0:T(2,128)S(1)} %add.12), channel_id=1, source_target_pairs={{0,2},{1,3},{2,0},{3,1},{4,6},{5,7},{6,4},{7,5},{8,10},{9,11},{10,... | collective-permute-start | bytes 3080 | tf_op jit(solution)/shard_map/ppermute | solution.py:316
  30.5 9.6 %collective-permute-start.15 = (bf16[128,1024]{1,0:T(8,128)(2,1)S(1)}, bf16[128,1024]{1,0:T(8,128)(2,1)S(1)}, u32[]{:S(2)}, u32[]{:S(2)}) collective-permute-start(bf16[128,1024]{1,0:T(8,128)(2,1)S(1)} %merge_k.1), channel_id=1, source_target_pairs={{2,0},{3,1},{4,2},{5,3},{6,4},{7,5},{10,8},{11,9},{12,10},{13,11},... | collective-permute-start | bytes 786440 | tf_op jit(solution)/shard_map/ppermute | solution.py:27
  31.8 3.6 %collective-permute-start.13 = (f32[2,128]{1,0:T(2,128)S(1)}, f32[2,128]{1,0:T(2,128)S(1)}, u32[]{:S(2)}, u32[]{:S(2)}) collective-permute-start(f32[2,128]{1,0:T(2,128)S(1)} %add.13), channel_id=1, source_target_pairs={{0,8},{8,0},{16,24},{24,16},{1,9},{9,1},{17,25},{25,17},{2,10},{10... | collective-permute-start | bytes 3080 | tf_op jit(solution)/shard_map/ppermute | solution.py:316
  35.5 3.6 %collective-permute-start.14 = (f32[2,128]{1,0:T(2,128)S(1)}, f32[2,128]{1,0:T(2,128)S(1)}, u32[]{:S(2)}, u32[]{:S(2)}) collective-permute-start(f32[2,128]{1,0:T(2,128)S(1)} %add.14), channel_id=1, source_target_pairs={{0,16},{8,24},{16,0},{24,8},{1,17},{9,25},{17,1},{25,9},{2,18},{10... | collective-permute-start | bytes 3080 | tf_op jit(solution)/shard_map/ppermute | solution.py:316
  40.1 4.5 %collective-permute-start.16 = (f32[2,128]{1,0:T(2,128)S(1)}, f32[2,128]{1,0:T(2,128)S(1)}, u32[]{:S(2)}, u32[]{:S(2)}) collective-permute-start(f32[2,128]{1,0:T(2,128)S(1)} %add.15.own_ref), channel_id=1, source_target_pairs={{0,4},{1,5},{2,6},{3,7},{4,0},{5,1},{6,2},{7,3},{8,12},{9,13},{10,... | collective-permute-start | bytes 3080 | tf_op jit(solution)/shard_map/ppermute | solution.py:316
